TPU v7x, 32 devices: a whole 2x2x4 slice. The times are simulated.
32 devices in a mesh: row: 8 (over z, y), col: 4 (over x, core).
Axes of the slice: x: 2, y: 2, z: 4, core: 2. Of those that a mesh axis runs over, the one named last changes fastest.
Arguments:
- ancestor_inverse: float32 [12288, 12288], P('row', 'col'), may hold values from -5 to 320, as said below
- panel_one: float32 [12288, 256], P(('row', 'col')), may hold values from -0.015625 to 0.015625
- struct_one: int32 [10752], replicated, may hold values from 0 to 12287, as said below
- lower_one: float32 [256, 256], replicated, may hold values from -1 to 2, as said below
- panel_two: float32 [12288, 256], P(('row', 'col')), may hold values from -0.015625 to 0.015625
- struct_two: int32 [9216], replicated, may hold values from 0 to 12287, as said below
- panel_above: float32 [256, 256], replicated, may hold values from -0.375 to 0.375
- lower_two: float32 [256, 256], replicated, may hold values from -1 to 2, as said below
- tile_owner: int32 [192, 1], P(('col', 'row')), may hold values from 0 to 3; in each aligned block of 6 rows (0 to 5, 6 to 11, ...) at most 2 rows name the same one
Outputs:
- inverse_one: float32 [12288, 256], P(('col', 'row'))
- diag_one: float32 [256, 256], replicated
- cross_two: float32 [256, 256], replicated
- diag_two: float32 [256, 256], replicated
- delivered: float32 [256, 64, 256], P(('row', 'col'))
Inputs may be any that keep to these rules, and one draw needn't show every extreme that they name: ancestor_inverse is exactly symmetric and positive definite. `struct_one`: 10752 distinct row numbers of the ancestor block. `struct_two`: 9216 distinct entries of struct_one. `lower_one`: lower triangular with a positive diagonal. `lower_two`: lower triangular with a positive diagonal. `tile_owner`: within each aligned block of 6 entries (the tiles of one device) no value appears more than 2 times; in some block a value appears exactly 2 times.
All inputs are finite; a program needn't handle non-finite values.
Results may differ from a plain program's by a relative error of at most 0.00007.
Values sent between devices are 32-bit elements; how exact they have to be, the bound alone decides.
A program may use at most 64 MiB of HBM per device.

v0:
```python
import functools

import jax
import jax.numpy as jnp
from jax import lax
from jax.experimental import pallas as pl
from jax.experimental.pallas import tpu as pltpu
from jax.sharding import PartitionSpec as P

CAP = 2


def matmul(left, right):
    return jnp.dot(left, right, precision=lax.Precision.HIGHEST, preferred_element_type=jnp.float32)


def contract_rows(left, right, precision=lax.Precision.HIGHEST):
    return lax.dot_general(
        left,
        right,
        (((0,), (0,)), ((), ())),
        precision=precision,
        preferred_element_type=jnp.float32,
    )


def row_mask(struct, count):
    lanes = 128
    high = struct // lanes
    low = struct % lanes
    high_hot = (jnp.arange(count // lanes, dtype=jnp.int32)[:, None] == high[None, :]).astype(jnp.bfloat16)
    low_hot = (jnp.arange(lanes, dtype=jnp.int32)[:, None] == low[None, :]).astype(jnp.bfloat16)
    counts = lax.dot_general(high_hot, low_hot, (((1,), (1,)), ((), ())), preferred_element_type=jnp.float32)
    return (counts > 0.5).astype(jnp.float32).reshape(count)


MESH = pl.DeviceIdType.MESH


def greet(peers):
    barrier = pltpu.get_barrier_semaphore()
    for peer in peers:
        pl.semaphore_signal(barrier, inc=1, device_id=peer, device_id_type=MESH)
    pl.semaphore_wait(barrier, len(peers))


def scatter_kernel(rows, value_ref, out_ref, pair_in, total, major_in, pair_send, pair_recv, major_send, major_recv):
    majors = rows // 2
    row = lax.axis_index("row")
    col = lax.axis_index("col")
    major, minor = row // 2, row % 2
    partner = (major * 2 + 1 - minor, col)

    def peer(offset):
        return (lax.rem(major + offset, majors) * 2 + minor, col)

    greet([partner] + [peer(offset) for offset in range(1, majors)])
    order = sorted(range(1, majors), key=lambda offset: -min(offset, majors - offset)) + [0]
    started = []
    pair_copies = {}
    for offset in order:
        target = lax.rem(major + offset, majors)
        copy = pltpu.make_async_remote_copy(
            src_ref=value_ref.at[target * 2 + 1 - minor],
            dst_ref=pair_in.at[offset],
            send_sem=pair_send.at[offset],
            recv_sem=pair_recv.at[offset],
            device_id=partner,
            device_id_type=MESH,
        )
        copy.start()
        pair_copies[offset] = copy
    for offset in order:
        target = lax.rem(major + offset, majors)
        pair_copies[offset].wait_recv()
        total[offset] = pair_in[offset] + value_ref[target * 2 + minor]
        if offset:
            copy = pltpu.make_async_remote_copy(
                src_ref=total.at[offset],
                dst_ref=major_in.at[offset - 1],
                send_sem=major_send.at[offset - 1],
                recv_sem=major_recv.at[offset - 1],
                device_id=peer(offset),
                device_id_type=MESH,
            )
            copy.start()
            started.append(copy)
    for copy in started:
        copy.wait_recv()
    result = total[0]
    for slot in range(majors - 1):
        result = result + major_in[slot]
    out_ref[...] = result
    for copy in started:
        copy.wait_send()
    for offset in order:
        pair_copies[offset].wait_send()


def scatter_rows(value, rows):
    chunk, width = value.shape[0] // rows, value.shape[1]
    majors = rows // 2
    dma = pltpu.SemaphoreType.DMA
    return pl.pallas_call(
        functools.partial(scatter_kernel, rows),
        out_shape=jax.ShapeDtypeStruct((chunk, width), jnp.float32),
        in_specs=[pl.BlockSpec(memory_space=pltpu.VMEM)],
        out_specs=pl.BlockSpec(memory_space=pltpu.VMEM),
        scratch_shapes=[
            pltpu.VMEM((majors, chunk, width), jnp.float32),
            pltpu.VMEM((majors, chunk, width), jnp.float32),
            pltpu.VMEM((majors - 1, chunk, width), jnp.float32),
            dma((majors,)),
            dma((majors,)),
            dma((majors - 1,)),
            dma((majors - 1,)),
        ],
        compiler_params=pltpu.CompilerParams(
            collective_id=0, has_side_effects=True, vmem_limit_bytes=40 * 2**20
        ),
    )(value.reshape(rows, chunk, width))


def gather_kernel(cols, parts, block_ref, high_ref, low_ref, held, pair_send, pair_recv, far_send, far_recv, relay_send, relay_recv):
    row = lax.axis_index("row")
    col = lax.axis_index("col")
    outer = cols // 2
    far, core = col // 2, col % 2
    partner = (row, far * 2 + 1 - core)

    def far_peer(offset):
        return (row, lax.rem(far + offset, outer) * 2 + core)

    greet([partner] + [far_peer(offset) for offset in range(1, outer)])

    def send(source, slot, part, target, send_sem, recv_sem):
        copy = pltpu.make_async_remote_copy(
            src_ref=source,
            dst_ref=held.at[slot, part],
            send_sem=send_sem,
            recv_sem=recv_sem,
            device_id=target,
            device_id_type=MESH,
        )
        copy.start()
        return copy

    far_copies = [
        (offset, part, send(
            block_ref.at[part], col, part, far_peer(offset), far_send.at[offset - 1, part], far_recv.at[offset - 1, part]
        ))
        for part in range(parts)
        for offset in range(1, outer)
    ]
    pair_copies = [
        send(block_ref.at[part], col, part, partner, pair_send.at[part], pair_recv.at[part]) for part in range(parts)
    ]
    relays = []
    for offset, part, copy in far_copies:
        copy.wait_recv()
        source = lax.rem(far - offset + outer, outer) * 2 + core
        relays.append(
            send(
                held.at[source, part],
                source,
                part,
                partner,
                relay_send.at[offset - 1, part],
                relay_recv.at[offset - 1, part],
            )
        )
    held[col] = block_ref[...]
    for copy in pair_copies + relays:
        copy.wait_recv()
    height, length = block_ref.shape[1:]
    for slot in range(cols):
        for part in range(parts):
            value = held[slot, part]
            high = value.astype(jnp.bfloat16)
            place = (pl.ds(part * height, height), pl.ds(slot * length, length))
            high_ref[place] = high
            low_ref[place] = (value - high.astype(jnp.float32)).astype(jnp.bfloat16)
    for copy in pair_copies + relays + [entry[2] for entry in far_copies]:
        copy.wait_send()


def gather_columns(block, cols):
    parts = 2
    width, length = block.shape
    outer = cols // 2
    dma = pltpu.SemaphoreType.DMA
    return pl.pallas_call(
        functools.partial(gather_kernel, cols, parts),
        out_shape=[jax.ShapeDtypeStruct((width, cols * length), jnp.bfloat16)] * 2,
        in_specs=[pl.BlockSpec(memory_space=pltpu.VMEM)],
        out_specs=[pl.BlockSpec(memory_space=pltpu.VMEM)] * 2,
        scratch_shapes=[pltpu.VMEM((cols, parts, width // parts, length), jnp.float32)]
        + [dma((parts,))] * 2
        + [dma((outer - 1, parts))] * 4,
        compiler_params=pltpu.CompilerParams(
            collective_id=2, has_side_effects=True, vmem_limit_bytes=24 * 2**20
        ),
    )(block.reshape(parts, width // parts, length))


def product_kernel(
    rows, matrix_ref, high_ref, low_ref, out_ref, window, mine, other, pair_in, major_in,
    window_sem, pair_send, pair_recv, major_send, major_recv,
):
    majors = rows // 2
    row = lax.axis_index("row")
    col = lax.axis_index("col")
    major, minor = row // 2, row % 2
    partner = (major * 2 + 1 - minor, col)
    span = out_ref.shape[1]

    upper, lower = major // 2, major % 2
    near = ((upper * 2 + 1 - lower) * 2 + minor, col)
    away = (((1 - upper) * 2 + lower) * 2 + minor, col)

    def fetch(step, which):
        target_upper = lax.rem(upper + 1 + step // 2, 2)
        target_lower = lax.rem(lower + 1 + step, 2)
        target = (target_upper * 2 + target_lower) * 2 + lax.rem(1 - minor + which, 2)
        return pltpu.make_async_copy(
            matrix_ref.at[:, pl.ds(pl.multiple_of(target * span, 128), span)],
            window.at[which],
            window_sem.at[which],
        )

    def pair_copy(step):
        return pltpu.make_async_remote_copy(
            src_ref=other.at[step],
            dst_ref=pair_in.at[step],
            send_sem=pair_send.at[step],
            recv_sem=pair_recv.at[step],
            device_id=partner,
            device_id_type=MESH,
        )

    for which in range(2):
        fetch(0, which).start()
    greet([partner, near, away])

    def dot(left, right):
        return jnp.dot(left, right, preferred_element_type=jnp.float32)

    def body(step, carry):
        for which, result in enumerate((other, mine)):
            fetch(step, which).wait()
            value = window[which]
            high = value.astype(jnp.bfloat16)
            low = (value - high.astype(jnp.float32)).astype(jnp.bfloat16)
            result[step] = dot(high_ref[...], high) + (dot(high_ref[...], low) + dot(low_ref[...], high))

            @pl.when(step + 1 < majors)
            def _():
                fetch(step + 1, which).start()

            if which == 0:
                pair_copy(step).start()
        return carry

    lax.fori_loop(0, majors, body, 0)

    def forward(source, slot, target):
        copy = pltpu.make_async_remote_copy(
            src_ref=mine.at[source],
            dst_ref=major_in.at[slot],
            send_sem=major_send.at[slot],
            recv_sem=major_recv.at[slot],
            device_id=target,
            device_id_type=MESH,
        )
        copy.start()
        return copy

    pair_copy(0).wait_recv()
    mine[0] = mine[0] + pair_in[0]
    both_bits = forward(0, 0, near)
    pair_copy(1).wait_recv()
    mine[1] = mine[1] + pair_in[1]
    both_bits.wait_recv()
    mine[1] = mine[1] + major_in[0]
    high_bit = forward(1, 1, away)
    pair_copy(2).wait_recv()
    mine[2] = mine[2] + pair_in[2]
    low_bit = forward(2, 2, near)
    pair_copy(3).wait_recv()
    mine[3] = mine[3] + pair_in[3]
    high_bit.wait_recv()
    low_bit.wait_recv()
    out_ref[...] = mine[3] + major_in[1] + major_in[2]
    for copy in (both_bits, high_bit, low_bit):
        copy.wait_send()
    for step in range(majors):
        pair_copy(step).wait_send()


def product_rows(matrix, high, low, rows):
    width = high.shape[0]
    depth = matrix.shape[0]
    span = matrix.shape[1] // rows
    majors = rows // 2
    dma = pltpu.SemaphoreType.DMA
    vmem = lambda *shape: pltpu.VMEM(shape, jnp.float32)
    return pl.pallas_call(
        functools.partial(product_kernel, rows),
        out_shape=jax.ShapeDtypeStruct((width, span), jnp.float32),
        in_specs=[pl.BlockSpec(memory_space=pl.ANY)] + [pl.BlockSpec(memory_space=pltpu.VMEM)] * 2,
        out_specs=pl.BlockSpec(memory_space=pltpu.VMEM),
        scratch_shapes=[
            vmem(2, depth, span),
            vmem(majors, width, span),
            vmem(majors, width, span),
            vmem(majors, width, span),
            vmem(majors - 1, width, span),
            dma((2,)),
            dma((majors,)),
            dma((majors,)),
            dma((majors - 1,)),
            dma((majors - 1,)),
        ],
        compiler_params=pltpu.CompilerParams(
            collective_id=0, has_side_effects=True, vmem_limit_bytes=48 * 2**20
        ),
        cost_estimate=pl.CostEstimate(
            flops=6 * matrix.size * width, bytes_accessed=10 * matrix.size, transcendentals=0
        ),
    )(matrix, high, low)


def sum_kernel(rows, cols, value_ref, out_ref, full, sum_a, sum_b, in_a, in_b, in_c, *sems):
    row = lax.axis_index("row")
    col = lax.axis_index("col")
    outer = cols // 2
    far, core = col // 2, col % 2
    half = outer * rows
    base_a = core * half
    base_b = base_a + far * rows
    base_c = base_b + row

    def pair_peer(offset):
        return (row, far * 2 + 1 - core)

    def far_peer(offset):
        return (row, lax.rem(far + offset, outer) * 2 + core)

    def row_peer(offset):
        return (lax.rem(row + offset, rows), col)

    greet(
        [pair_peer(1)]
        + [far_peer(offset) for offset in range(1, outer)]
        + [row_peer(offset) for offset in range(1, rows)]
    )

    def exchange(count, peer, source, landing, stage):
        copies = []
        for offset in range(1, count):
            copy = pltpu.make_async_remote_copy(
                src_ref=source(offset),
                dst_ref=landing(offset),
                send_sem=sems[2 * stage].at[offset - 1],
                recv_sem=sems[2 * stage + 1].at[offset - 1],
                device_id=peer(offset),
                device_id_type=MESH,
            )
            copy.start()
            copies.append(copy)
        for copy in copies:
            copy.wait_recv()
        return copies

    pending = []
    pending += exchange(
        2, pair_peer, lambda k: value_ref.at[pl.ds((1 - core) * half, half)], lambda k: in_a.at[k - 1], 0
    )
    sum_a[...] = value_ref[pl.ds(base_a, half)] + in_a[0]
    pending += exchange(
        outer, far_peer, lambda k: sum_a.at[pl.ds(lax.rem(far + k, outer) * rows, rows)], lambda k: in_b.at[k - 1], 1
    )
    total = sum_a[pl.ds(far * rows, rows)]
    for slot in range(outer - 1):
        total = total + in_b[slot]
    sum_b[...] = total
    pending += exchange(
        rows, row_peer, lambda k: sum_b.at[lax.rem(row + k, rows)], lambda k: in_c.at[k - 1], 2
    )
    total = sum_b[row]
    for slot in range(rows - 1):
        total = total + in_c[slot]
    full[base_c] = total
    pending += exchange(rows, row_peer, lambda k: full.at[base_c], lambda k: full.at[base_c], 3)
    pending += exchange(
        outer, far_peer, lambda k: full.at[pl.ds(base_b, rows)], lambda k: full.at[pl.ds(base_b, rows)], 4
    )
    pending += exchange(
        2, pair_peer, lambda k: full.at[pl.ds(base_a, half)], lambda k: full.at[pl.ds(base_a, half)], 5
    )
    out_ref[...] = full[...]
    for copy in pending:
        copy.wait_send()


def sum_everywhere(value, rows, cols):
    devices = rows * cols
    lanes = value.shape[1]
    depth = value.shape[0] // devices
    outer = cols // 2
    dma = pltpu.SemaphoreType.DMA
    vmem = lambda *lead: pltpu.VMEM(lead + (depth, lanes), jnp.float32)
    total = pl.pallas_call(
        functools.partial(sum_kernel, rows, cols),
        out_shape=jax.ShapeDtypeStruct((devices, depth, lanes), jnp.float32),
        in_specs=[pl.BlockSpec(memory_space=pltpu.VMEM)],
        out_specs=pl.BlockSpec(memory_space=pltpu.VMEM),
        scratch_shapes=[
            vmem(devices),
            vmem(devices // 2),
            vmem(rows),
            vmem(1, devices // 2),
            vmem(outer - 1, rows),
            vmem(rows - 1),
        ]
        + [dma((count - 1,)) for count in (2, outer, rows, rows, outer, 2) for _ in range(2)],
        compiler_params=pltpu.CompilerParams(
            collective_id=1, has_side_effects=True, vmem_limit_bytes=24 * 2**20
        ),
        cost_estimate=pl.CostEstimate(flops=0, bytes_accessed=100 * value.size * 4, transcendentals=0),
    )(value.reshape(devices, depth, lanes))
    return total.reshape(value.shape)


def deliver(values, tile_owner, col_count):
    tile_count = tile_owner.shape[0]
    tile_rows = values.shape[0] // tile_count
    all_tiles = values.reshape(tile_count, tile_rows, values.shape[1])
    owner_col = tile_owner[:, 0]
    col_ids = jnp.arange(col_count, dtype=jnp.int32)
    onehot = (owner_col[:, None] == col_ids[None, :]).astype(jnp.int32)
    tile_rank = jnp.sum((jnp.cumsum(onehot, axis=0) - onehot) * onehot, axis=1)
    slot_index = jnp.arange(CAP, dtype=jnp.int32)
    select = (
        (owner_col[None, None, :] == col_ids[:, None, None])
        & (tile_rank[None, None, :] == slot_index[None, :, None])
    ).astype(jnp.float32)
    outgoing = jnp.einsum("cks,srb->ckrb", select, all_tiles, precision=lax.Precision.HIGHEST)
    incoming = lax.all_to_all(outgoing, "col", split_axis=0, concat_axis=0, tiled=True)
    return incoming.reshape(col_count * CAP, tile_rows, values.shape[1])


def local(
    ancestor_inverse,
    panel_one,
    struct_one,
    lower_one,
    panel_two,
    struct_two,
    panel_above,
    lower_two,
    tile_owner,
):
    row_count = lax.axis_size("row")
    col_count = lax.axis_size("col")
    row_index = lax.axis_index("row")
    col_index = lax.axis_index("col")
    local_rows = panel_one.shape[0]
    order = local_rows * row_count * col_count
    width = panel_one.shape[1]
    mask_one = row_mask(struct_one, order)
    mask_two = row_mask(struct_two, order)
    panel_start = (row_index * col_count + col_index) * local_rows
    result_start = (col_index * row_count + row_index) * local_rows
    local_one = panel_one * lax.dynamic_slice_in_dim(mask_one, panel_start, local_rows)[:, None]
    local_two = panel_two * lax.dynamic_slice_in_dim(mask_two, panel_start, local_rows)[:, None]
    result_mask_one = lax.dynamic_slice_in_dim(mask_one, result_start, local_rows)[:, None]
    result_mask_two = lax.dynamic_slice_in_dim(mask_two, result_start, local_rows)[:, None]

    both = jnp.concatenate([local_one, local_two], axis=1)
    late = both
    if local_rows % 128 == 0 and row_count // 2 == 4:
        high, low = gather_columns(both.T, col_count)
        high, late = lax.optimization_barrier((high, both))
        product = product_rows(ancestor_inverse, high, low, row_count).T
    else:
        gathered = lax.all_gather(both, "col", axis=0, tiled=True)
        product = scatter_rows(contract_rows(ancestor_inverse, gathered, lax.Precision.HIGH), row_count)
    moves = [(f, (f % row_count) * col_count + f // row_count) for f in range(row_count * col_count)]
    resident = lax.ppermute(late, ("row", "col"), moves)
    resident_one = resident[:, :width]
    resident_two = resident[:, width:]
    inverse_one = -product[:, :width] * result_mask_one
    inverse_two = -(product[:, width:] + matmul(inverse_one, panel_above)) * result_mask_two
    grams = (
        contract_rows(resident_one, inverse_one),
        contract_rows(inverse_one, resident_two),
        contract_rows(resident_two, inverse_two),
    )
    lanes = 128
    packed = jnp.concatenate(
        [gram[:, at : at + lanes] for gram in grams for at in range(0, width, lanes)], axis=0
    )
    sums = sum_everywhere(packed, row_count, col_count).reshape(len(grams), width // lanes, width, lanes)
    gram_one, cross_sum, gram_two = (
        jnp.concatenate([sums[at, block] for block in range(width // lanes)], axis=1) for at in range(len(grams))
    )
    diag_one = matmul(lower_one.T, lower_one) - gram_one
    cross_two = -(cross_sum + matmul(diag_one, panel_above))
    diag_two = matmul(lower_two.T, lower_two) - gram_two - matmul(panel_above.T, cross_two)
    delivered = deliver(inverse_two, tile_owner, col_count)
    return (inverse_one, diag_one, cross_two, diag_two, delivered)


def solution(mesh):
    return jax.shard_map(
        local,
        mesh=mesh,
        in_specs=(
            P("row", "col"),
            P(("row", "col"), None),
            P(),
            P(),
            P(("row", "col"), None),
            P(),
            P(),
            P(),
            P(("col", "row"), None),
        ),
        out_specs=(P(("col", "row"), None), P(), P(), P(), P(("row", "col"), None, None)),
        check_vma=False,
    )
```

profile of v0, /device:TPU:0, one launch (start us, length us, event | category | flops | bytes accessed | tf_op | source)
XLA Modules:
  0.0 201.8 jit_solution(742402828323211478)
XLA Ops:
  0.6 0.0 copy-start
  0.7 0.9 add_select_fusion.1
  1.6 0.8 add_select_fusion.3
  2.4 1.4 fusion.15
  3.8 1.3 fusion.12
  5.1 0.1 fusion.36
  5.2 0.1 broadcast_multiply_fusion
  5.3 0.1 broadcast_multiply_fusion.1
  5.5 0.2 pad_maximum_fusion
  5.7 0.3 copy.33
  5.9 23.0 %shard_map.128 = (bf16[512,1536]{1,0:T(8,128)(2,1)S(1)}, bf16[512,1536]{1,0:T(8,128)(2,1)S(1)}) custom-call(f32[2,256,384]{2,1,0:T(8,128)S(1)} %bitcast.51), custom_call_target="tpu_custom_call" | custom-call | tf_op jit(solution)/shard_map/pallas_call | solution.py:192
  29.0 0.7 collective-permute-start
  29.7 122.0 %shard_map.129 = f32[512,384]{1,0:T(8,128)S(1)} custom-call(f32[1536,3072]{1,0:T(8,128)} %matrix_ref.1, bf16[512,1536]{1,0:T(8,128)(2,1)S(1)} %get-tuple-element.10.high_ref, bf16[512,1536]{1,0:T(8,128)(2,1)S(1)} %get-tuple-element.11.low_ref), custom_call_target="tpu_custom_call" | custom-call | flops 14495514624 | bytes 47185920 | tf_op jit(solution)/shard_map/pallas_call | solution.py:307
  151.8 0.6 fusion.7
  152.4 0.2 copy.36
  152.6 0.2 reduce_window_sum.11
  152.8 0.7 fusion.16
  153.5 0.9 copy.38
  154.4 3.7 %all-to-all-start = ((f32[4,2,64,256]{3,2,1,0:T(8,128)}), f32[4,2,64,256]{3,2,1,0:T(8,128)S(1)}, u32[]{:S(2)}, u32[]{:S(2)}) async-start(f32[4,2,64,256]{3,2,1,0:T(8,128)} %copy.38), calls=%async_computation | async-start | bytes 1048576 | tf_op jit(solution)/shard_map/all_to_all | solution.py:449
  158.0 0.9 copy.39
  159.0 7.7 %all-to-all-done = f32[4,2,64,256]{3,2,1,0:T(8,128)S(1)} async-done(((f32[4,2,64,256]{3,2,1,0:T(8,128)}), f32[4,2,64,256]{3,2,1,0:T(8,128)S(1)}, u32[]{:S(2)}, u32[]{:S(2)}) %all-to-all-start) | async-done | bytes 524320 | tf_op jit(solution)/shard_map/all_to_all | solution.py:449
  166.7 0.8 fusion.19
  167.5 0.6 fusion.24
  168.2 0.8 fusion.22
  169.0 29.0 %shard_map.130 = f32[32,48,128]{2,1,0:T(8,128)S(1)} custom-call(f32[32,48,128]{2,1,0:T(8,128)S(1)} %bitcast.52), custom_call_target="tpu_custom_call" | custom-call | bytes 78643200 | tf_op jit(solution)/shard_map/pallas_call | solution.py:413
  198.0 0.1 slice_bitcast_fusion.1
  198.1 0.6 convolution_subtract_fusion
  198.7 0.6 convolution_subtract_fusion.1
  199.3 0.0 copy-start.3
  199.3 0.4 fusion.9
  199.7 1.3 fusion.8
  201.0 0.8 copy.53
  (26 shorter events, 0.2 us)
Async XLA Ops:
  0.6 151.1 %copy-start = (f32[256,256]{1,0:T(8,128)S(1)}, f32[256,256]{1,0:T(8,128)}, u32[]{:S(2)}) copy-start(f32[256,256]{1,0:T(8,128)} %param.15) | copy-start | bytes 786436
  0.6 4.6 %copy-start.5 = (f32[384,256]{1,0:T(8,128)S(1)}, f32[384,256]{1,0:T(8,128)}, u32[]{:S(2)}) copy-start(f32[384,256]{1,0:T(8,128)} %param.13) | copy-start | bytes 1179652
  0.7 4.7 %copy-start.6 = (f32[384,256]{1,0:T(8,128)S(1)}, f32[384,256]{1,0:T(8,128)}, u32[]{:S(2)}) copy-start(f32[384,256]{1,0:T(8,128)} %param.10) | copy-start | bytes 1179652
  5.1 24.6 %copy-start.7 = (s32[6,1]{0,1:T(1,128)S(1)}, s32[6,1]{0,1:T(1,128)}, u32[]{:S(2)}) copy-start(s32[6,1]{0,1:T(1,128)} %param.17) | copy-start | bytes 76
  29.0 137.7 %collective-permute-start = (f32[384,512]{1,0:T(8,128)S(1)}, f32[384,512]{1,0:T(8,128)S(1)}, u32[]{:S(2)}, u32[]{:S(2)}) collective-permute-start(f32[384,512]{1,0:T(8,128)S(1)} %get-tuple-element.12), channel_id=1, source_target_pairs={{0,0},{1,4},{2,8},{3,12},{4,16},{5,20},{6,24},{7,28},{8,1},{9,5},{... | collective-permute-start | bytes 2359304 | tf_op jit(solution)/shard_map/ppermute | solution.py:490
  154.4 12.3 %all-to-all-start = ((f32[4,2,64,256]{3,2,1,0:T(8,128)}), f32[4,2,64,256]{3,2,1,0:T(8,128)S(1)}, u32[]{:S(2)}, u32[]{:S(2)}) async-start(f32[4,2,64,256]{3,2,1,0:T(8,128)} %copy.38), calls=%async_computation | async-start | bytes 1048576 | tf_op jit(solution)/shard_map/all_to_all | solution.py:449
  167.5 30.6 %copy-start.1 = (f32[256,256]{1,0:T(8,128)S(1)}, f32[256,256]{1,0:T(8,128)}, u32[]{:S(2)}) copy-start(f32[256,256]{1,0:T(8,128)} %param.16) | copy-start | bytes 786436
  167.5 31.2 %copy-start.2 = (f32[256,256]{1,0:T(8,128)S(1)}, f32[256,256]{1,0:T(8,128)}, u32[]{:S(2)}) copy-start(f32[256,256]{1,0:T(8,128)} %param.12) | copy-start | bytes 786436
  199.3 2.5 %copy-start.3 = (f32[256,256]{1,0:T(8,128)}, f32[256,256]{1,0:T(8,128)S(1)}, u32[]{:S(2)}) copy-start(f32[256,256]{1,0:T(8,128)S(1)} %convolution_subtract_fusion.1) | copy-start | bytes 786436
  199.7 2.1 %copy-start.4 = (f32[256,256]{1,0:T(8,128)}, f32[256,256]{1,0:T(8,128)S(1)}, u32[]{:S(2)}) copy-start(f32[256,256]{1,0:T(8,128)S(1)} %fusion.9) | copy-start | bytes 786436
where the time goes:
time: 202 us
  Pallas kernels  174 us (86%)
  matrix products  9.08 us (4%)
  waiting for transfers between devices  7.69 us (4%)
  starting transfers between devices  4.36 us (2%)
  local copies, waits for them, and re-layouts  3.29 us (2%)
  other arithmetic  2.4 us (1%)
    pallas_call x1, Pallas kernels, product_rows(): pl.pallas_call(functools.partial(product_kernel, rows), out_shape=jax.Sha...  122 us
    pallas_call x1, Pallas kernels, sum_everywhere(): pl.pallas_call(functools.partial(sum_kernel, rows, cols), out_shape=jax.S...  29 us
    pallas_call x1, Pallas kernels, gather_columns(): pl.pallas_call(functools.partial(gather_kernel, cols, parts), out_shape=[...  23 us
    all_to_all x1, waiting for transfers between devices, deliver(): lax.all_to_all(outgoing, 'col', split_axis=0, concat_axis=0, tiled=True)  7.68 us
  transfers between devices with their start and end apart: 2, of which 1 were waited for; matrix products, arithmetic and copies ran while one was open for 2% of the time, Pallas kernels for 60%

commit v1 on v0

--- a/solution.py
+++ b/solution.py
@@ -121,215 +121,6 @@
     )(value.reshape(rows, chunk, width))
 
 
-def gather_kernel(cols, parts, block_ref, high_ref, low_ref, held, pair_send, pair_recv, far_send, far_recv, relay_send, relay_recv):
-    row = lax.axis_index("row")
-    col = lax.axis_index("col")
-    outer = cols // 2
-    far, core = col // 2, col % 2
-    partner = (row, far * 2 + 1 - core)
-
-    def far_peer(offset):
-        return (row, lax.rem(far + offset, outer) * 2 + core)
-
-    greet([partner] + [far_peer(offset) for offset in range(1, outer)])
-
-    def send(source, slot, part, target, send_sem, recv_sem):
-        copy = pltpu.make_async_remote_copy(
-            src_ref=source,
-            dst_ref=held.at[slot, part],
-            send_sem=send_sem,
-            recv_sem=recv_sem,
-            device_id=target,
-            device_id_type=MESH,
-        )
-        copy.start()
-        return copy
-
-    far_copies = [
-        (offset, part, send(
-            block_ref.at[part], col, part, far_peer(offset), far_send.at[offset - 1, part], far_recv.at[offset - 1, part]
-        ))
-        for part in range(parts)
-        for offset in range(1, outer)
-    ]
-    pair_copies = [
-        send(block_ref.at[part], col, part, partner, pair_send.at[part], pair_recv.at[part]) for part in range(parts)
-    ]
-    relays = []
-    for offset, part, copy in far_copies:
-        copy.wait_recv()
-        source = lax.rem(far - offset + outer, outer) * 2 + core
-        relays.append(
-            send(
-                held.at[source, part],
-                source,
-                part,
-                partner,
-                relay_send.at[offset - 1, part],
-                relay_recv.at[offset - 1, part],
-            )
-        )
-    held[col] = block_ref[...]
-    for copy in pair_copies + relays:
-        copy.wait_recv()
-    height, length = block_ref.shape[1:]
-    for slot in range(cols):
-        for part in range(parts):
-            value = held[slot, part]
-            high = value.astype(jnp.bfloat16)
-            place = (pl.ds(part * height, height), pl.ds(slot * length, length))
-            high_ref[place] = high
-            low_ref[place] = (value - high.astype(jnp.float32)).astype(jnp.bfloat16)
-    for copy in pair_copies + relays + [entry[2] for entry in far_copies]:
-        copy.wait_send()
-
-
-def gather_columns(block, cols):
-    parts = 2
-    width, length = block.shape
-    outer = cols // 2
-    dma = pltpu.SemaphoreType.DMA
-    return pl.pallas_call(
-        functools.partial(gather_kernel, cols, parts),
-        out_shape=[jax.ShapeDtypeStruct((width, cols * length), jnp.bfloat16)] * 2,
-        in_specs=[pl.BlockSpec(memory_space=pltpu.VMEM)],
-        out_specs=[pl.BlockSpec(memory_space=pltpu.VMEM)] * 2,
-        scratch_shapes=[pltpu.VMEM((cols, parts, width // parts, length), jnp.float32)]
-        + [dma((parts,))] * 2
-        + [dma((outer - 1, parts))] * 4,
-        compiler_params=pltpu.CompilerParams(
-            collective_id=2, has_side_effects=True, vmem_limit_bytes=24 * 2**20
-        ),
-    )(block.reshape(parts, width // parts, length))
-
-
-def product_kernel(
-    rows, matrix_ref, high_ref, low_ref, out_ref, window, mine, other, pair_in, major_in,
-    window_sem, pair_send, pair_recv, major_send, major_recv,
-):
-    majors = rows // 2
-    row = lax.axis_index("row")
-    col = lax.axis_index("col")
-    major, minor = row // 2, row % 2
-    partner = (major * 2 + 1 - minor, col)
-    span = out_ref.shape[1]
-
-    upper, lower = major // 2, major % 2
-    near = ((upper * 2 + 1 - lower) * 2 + minor, col)
-    away = (((1 - upper) * 2 + lower) * 2 + minor, col)
-
-    def fetch(step, which):
-        target_upper = lax.rem(upper + 1 + step // 2, 2)
-        target_lower = lax.rem(lower + 1 + step, 2)
-        target = (target_upper * 2 + target_lower) * 2 + lax.rem(1 - minor + which, 2)
-        return pltpu.make_async_copy(
-            matrix_ref.at[:, pl.ds(pl.multiple_of(target * span, 128), span)],
-            window.at[which],
-            window_sem.at[which],
-        )
-
-    def pair_copy(step):
-        return pltpu.make_async_remote_copy(
-            src_ref=other.at[step],
-            dst_ref=pair_in.at[step],
-            send_sem=pair_send.at[step],
-            recv_sem=pair_recv.at[step],
-            device_id=partner,
-            device_id_type=MESH,
-        )
-
-    for which in range(2):
-        fetch(0, which).start()
-    greet([partner, near, away])
-
-    def dot(left, right):
-        return jnp.dot(left, right, preferred_element_type=jnp.float32)
-
-    def body(step, carry):
-        for which, result in enumerate((other, mine)):
-            fetch(step, which).wait()
-            value = window[which]
-            high = value.astype(jnp.bfloat16)
-            low = (value - high.astype(jnp.float32)).astype(jnp.bfloat16)
-            result[step] = dot(high_ref[...], high) + (dot(high_ref[...], low) + dot(low_ref[...], high))
-
-            @pl.when(step + 1 < majors)
-            def _():
-                fetch(step + 1, which).start()
-
-            if which == 0:
-                pair_copy(step).start()
-        return carry
-
-    lax.fori_loop(0, majors, body, 0)
-
-    def forward(source, slot, target):
-        copy = pltpu.make_async_remote_copy(
-            src_ref=mine.at[source],
-            dst_ref=major_in.at[slot],
-            send_sem=major_send.at[slot],
-            recv_sem=major_recv.at[slot],
-            device_id=target,
-            device_id_type=MESH,
-        )
-        copy.start()
-        return copy
-
-    pair_copy(0).wait_recv()
-    mine[0] = mine[0] + pair_in[0]
-    both_bits = forward(0, 0, near)
-    pair_copy(1).wait_recv()
-    mine[1] = mine[1] + pair_in[1]
-    both_bits.wait_recv()
-    mine[1] = mine[1] + major_in[0]
-    high_bit = forward(1, 1, away)
-    pair_copy(2).wait_recv()
-    mine[2] = mine[2] + pair_in[2]
-    low_bit = forward(2, 2, near)
-    pair_copy(3).wait_recv()
-    mine[3] = mine[3] + pair_in[3]
-    high_bit.wait_recv()
-    low_bit.wait_recv()
-    out_ref[...] = mine[3] + major_in[1] + major_in[2]
-    for copy in (both_bits, high_bit, low_bit):
-        copy.wait_send()
-    for step in range(majors):
-        pair_copy(step).wait_send()
-
-
-def product_rows(matrix, high, low, rows):
-    width = high.shape[0]
-    depth = matrix.shape[0]
-    span = matrix.shape[1] // rows
-    majors = rows // 2
-    dma = pltpu.SemaphoreType.DMA
-    vmem = lambda *shape: pltpu.VMEM(shape, jnp.float32)
-    return pl.pallas_call(
-        functools.partial(product_kernel, rows),
-        out_shape=jax.ShapeDtypeStruct((width, span), jnp.float32),
-        in_specs=[pl.BlockSpec(memory_space=pl.ANY)] + [pl.BlockSpec(memory_space=pltpu.VMEM)] * 2,
-        out_specs=pl.BlockSpec(memory_space=pltpu.VMEM),
-        scratch_shapes=[
-            vmem(2, depth, span),
-            vmem(majors, width, span),
-            vmem(majors, width, span),
-            vmem(majors, width, span),
-            vmem(majors - 1, width, span),
-            dma((2,)),
-            dma((majors,)),
-            dma((majors,)),
-            dma((majors - 1,)),
-            dma((majors - 1,)),
-        ],
-        compiler_params=pltpu.CompilerParams(
-            collective_id=0, has_side_effects=True, vmem_limit_bytes=48 * 2**20
-        ),
-        cost_estimate=pl.CostEstimate(
-            flops=6 * matrix.size * width, bytes_accessed=10 * matrix.size, transcendentals=0
-        ),
-    )(matrix, high, low)
-
-
 def sum_kernel(rows, cols, value_ref, out_ref, full, sum_a, sum_b, in_a, in_b, in_c, *sems):
     row = lax.axis_index("row")
     col = lax.axis_index("col")
@@ -450,6 +241,443 @@
     return incoming.reshape(col_count * CAP, tile_rows, values.shape[1])
 
 
+ROWS, COLS, CHIPS = 8, 4, 16
+CHUNKS = 4
+LANES = 128
+
+
+def fits_fused(matrix, panel, struct_one, struct_two, tile_owner, rows, cols):
+    span, width = panel.shape
+    return (
+        (rows, cols) == (ROWS, COLS)
+        and span % LANES == 0
+        and width == 2 * LANES
+        and matrix.shape == (cols * span, rows * span)
+        and struct_one.shape[0] % LANES == 0
+        and struct_two.shape[0] % LANES == 0
+        and span % (8 * tile_owner.shape[0]) == 0
+    )
+
+
+def exact(left, right, contract):
+    return lax.dot_general(
+        left, right, (contract, ((), ())), precision=lax.Precision.HIGHEST, preferred_element_type=jnp.float32
+    )
+
+
+def fused_kernel(
+    matrix, panel_one, panel_two, struct_one, struct_two, lower_one, above, lower_two, owner,
+    inverse_one, diag_one, cross_two, diag_two, delivered,
+    window, high, low, own, land, left, other, mine, pair_in, major_in, masks, resident, product,
+    packed, fold_in, fold, part_in, full, outgoing,
+    fetch_sem, own_sem, move_sem, near_gather, far_gather, relay_gather, pair_sem, major_sem, sum_sem, chip_sem,
+    spread_sem, tile_sem,
+):
+    row = lax.axis_index("row")
+    col = lax.axis_index("col")
+    z, y = row // 2, row % 2
+    x, core = col // 2, col % 2
+    upper, lower = z // 2, z % 2
+    chip = (z * 2 + y) * 2 + x
+    depth, total_columns = matrix.shape
+    span, width = own.shape[1:]
+    chunk = left.shape[1] // 2
+    per_panel = width // chunk
+
+    def device(z_at, y_at, x_at, core_at):
+        return (z_at * 2 + y_at, x_at * 2 + core_at)
+
+    partner = device(z, y, x, 1 - core)
+    across = device(z, y, 1 - x, core)
+    beside = device(z, 1 - y, x, core)
+    near = device(upper * 2 + 1 - lower, y, x, core)
+    away = device((1 - upper) * 2 + lower, y, x, core)
+
+    def remote(source, target, sems, at, peer):
+        return pltpu.make_async_remote_copy(
+            src_ref=source,
+            dst_ref=target,
+            send_sem=sems.at[(0,) + at],
+            recv_sem=sems.at[(1,) + at],
+            device_id=peer,
+            device_id_type=MESH,
+        )
+
+    own_copies = [
+        pltpu.make_async_copy(panel, own.at[at], own_sem.at[at]) for at, panel in enumerate((panel_one, panel_two))
+    ]
+    for copy in own_copies:
+        copy.start()
+
+    def fetch(step, which):
+        target_upper = lax.rem(upper + 1 + step // 2, 2)
+        target_lower = lax.rem(lower + 1 + step, 2)
+        target = (target_upper * 2 + target_lower) * 2 + lax.rem(1 - y + which, 2)
+        return pltpu.make_async_copy(
+            matrix.at[:, pl.ds(pl.multiple_of(target * span, LANES), span)], window.at[which], fetch_sem.at[which]
+        )
+
+    barrier = pltpu.get_barrier_semaphore()
+    devices = ROWS * COLS
+    for offset in range(1, devices):
+        flat = lax.rem(row * COLS + col + offset, devices)
+        pl.semaphore_signal(barrier, inc=1, device_id=(flat // COLS, lax.rem(flat, COLS)), device_id_type=MESH)
+    for which in range(2):
+        fetch(0, which).start()
+    pl.semaphore_wait(barrier, devices - 1)
+    for copy in own_copies:
+        copy.wait()
+
+    def piece(at):
+        return own.at[at // per_panel, :, pl.ds(at % per_panel * chunk, chunk)]
+
+    def far_copy(at, source=None):
+        return remote(land.at[0, at] if source is None else source, land.at[col, at], far_gather, (at,), across)
+
+    def near_copy(at, source=None):
+        return remote(land.at[0, at] if source is None else source, land.at[col, at], near_gather, (at,), partner)
+
+    def relay_copy(at):
+        slot = (1 - x) * 2 + core
+        return remote(land.at[slot, at], land.at[slot, at], relay_gather, (at,), partner)
+
+    place = row * COLS + col
+    move_row, move_col = lax.rem(place, ROWS), place // ROWS
+    stays = (move_row == row) & (move_col == col)
+    moved = remote(own, resident, move_sem, (), (move_row, move_col))
+    kept = pltpu.make_async_copy(own, resident, move_sem.at[1])
+    for at in range(CHUNKS):
+        far_copy(at, piece(at)).start()
+        near_copy(at, piece(at)).start()
+        if at == 0:
+            pl.when(stays)(lambda: kept.start())
+            pl.when(jnp.logical_not(stays))(lambda: moved.start())
+    for at in range(CHUNKS):
+        land[col, at] = piece(at)[...]
+
+    blocks = span // LANES
+    slots_of = COLS * blocks
+    mask_rows = masks.shape[1]
+    place_rows = lax.broadcasted_iota(jnp.int32, (mask_rows, LANES), 0)
+    block_base = row * slots_of
+    result_base = (col * ROWS + row) * blocks
+    wanted = jnp.where(place_rows < slots_of, block_base + place_rows, result_base + place_rows - slots_of)
+    lane_ids = lax.broadcasted_iota(jnp.int32, (LANES, LANES), 0)
+    for at, struct in enumerate((struct_one, struct_two)):
+        count = struct.shape[0]
+        group = max(size for size in range(1, 17) if count % size == 0)
+        counts = jnp.zeros((mask_rows, LANES), jnp.float32)
+        for begin in range(0, count, group):
+            highs, lows = [], []
+            for entry in range(begin, begin + group):
+                value = struct[pl.ds(entry, 1), :]
+                highs.append(jnp.where(wanted == value // LANES, 1.0, 0.0))
+                lows.append(jnp.where(lane_ids == value % LANES, 1.0, 0.0))
+            counts = counts + lax.dot_general(
+                jnp.concatenate(highs, axis=1).astype(jnp.bfloat16),
+                jnp.concatenate(lows, axis=1).astype(jnp.bfloat16),
+                (((1,), (1,)), ((), ())),
+                preferred_element_type=jnp.float32,
+            )
+        masks[at] = jnp.where(counts > 0.5, 1.0, 0.0)
+    diag_one[...] = exact(lower_one[...].T, lower_one[...], ((1,), (0,)))
+    diag_two[...] = exact(lower_two[...].T, lower_two[...], ((1,), (0,)))
+
+    def mask_of(panel, begin):
+        return jnp.concatenate([masks[panel, pl.ds(begin + at, 1), :] for at in range(blocks)], axis=1)
+
+    def prepare(at):
+        near_copy(at).wait_recv()
+        far_copy(at).wait_recv()
+        relay_copy(at).start()
+        relay_copy(at).wait_recv()
+        for slot in range(COLS):
+            value = land[slot, at].T * mask_of(at // per_panel, slot * blocks)
+            upper_part = value.astype(jnp.bfloat16)
+            columns = pl.ds(slot * span, span)
+            left[at, pl.ds(0, chunk), columns] = upper_part
+            left[at, pl.ds(chunk, chunk), columns] = (value - upper_part.astype(jnp.float32)).astype(jnp.bfloat16)
+
+    def pair_copy(at, step):
+        return remote(other.at[at, step], pair_in.at[at, step], pair_sem, (at, step), beside)
+
+    def multiply(at, step, which):
+        target = step * 2 + which
+        both = jnp.dot(left[at], high[target], preferred_element_type=jnp.float32)
+        rest = jnp.dot(left[at, pl.ds(0, chunk), :], low[target], preferred_element_type=jnp.float32)
+        value = both[:chunk] + (both[chunk:] + rest)
+        if which == 0:
+            other[at, step] = value
+            pair_copy(at, step).start()
+        else:
+            mine[at, step] = value
+
+    def first_step(step, carry):
+        for which in range(2):
+            fetch(step, which).wait()
+            target = step * 2 + which
+            for begin in range(0, depth, 256):
+                size = min(256, depth - begin)
+                value = window[which, pl.ds(begin, size), :]
+                upper_part = value.astype(jnp.bfloat16)
+                high[target, pl.ds(begin, size), :] = upper_part
+                low[target, pl.ds(begin, size), :] = (value - upper_part.astype(jnp.float32)).astype(jnp.bfloat16)
+
+            @pl.when(step + 1 < 4)
+            def _():
+                fetch(step + 1, which).start()
+
+            multiply(0, step, which)
+        return carry
+
+    def later_steps(at):
+        def body(step, carry):
+            for which in range(2):
+                multiply(at, step, which)
+            return carry
+
+        lax.fori_loop(0, 4, body, 0)
+
+    def major_copy(at, slot, peer):
+        return remote(mine.at[at, slot], major_in.at[at, slot], major_sem, (at, slot), peer)
+
+    def collect(at):
+        pair_copy(at, 0).wait_recv()
+        mine[at, 0] = mine[at, 0] + pair_in[at, 0]
+        major_copy(at, 0, near).start()
+        pair_copy(at, 1).wait_recv()
+        mine[at, 1] = mine[at, 1] + pair_in[at, 1]
+        major_copy(at, 0, near).wait_recv()
+        mine[at, 1] = mine[at, 1] + major_in[at, 0]
+        major_copy(at, 1, away).start()
+        pair_copy(at, 2).wait_recv()
+        mine[at, 2] = mine[at, 2] + pair_in[at, 2]
+        major_copy(at, 2, near).start()
+        pair_copy(at, 3).wait_recv()
+        value = mine[at, 3] + pair_in[at, 3]
+        major_copy(at, 1, away).wait_recv()
+        major_copy(at, 2, near).wait_recv()
+        product[at] = value + (major_in[at, 1] + major_in[at, 2])
+
+    prepare(0)
+    lax.fori_loop(0, 4, first_step, 0)
+
+    def rest_of(at, carry):
+        prepare(at)
+        later_steps(at)
+        collect(at - 1)
+        return carry
+
+    lax.fori_loop(1, CHUNKS, rest_of, 0)
+    collect(CHUNKS - 1)
+
+    one_row = mask_of(0, slots_of)
+    two_row = mask_of(1, slots_of)
+    inv_one_t = -(jnp.concatenate([product[at] for at in range(per_panel)], axis=0) * one_row)
+    part_two_t = -(jnp.concatenate([product[at] for at in range(per_panel, CHUNKS)], axis=0) * two_row)
+    moved.wait_recv()
+    last = ((1,), (1,))
+    panel_one_t = resident[0].T
+    panel_two_t = resident[1].T
+    gram_one = exact(panel_one_t, inv_one_t, last)
+    cross_sum = exact(inv_one_t * two_row, panel_two_t, last)
+    gram_two = exact(panel_two_t, part_two_t, last)
+    half = width // 2
+
+    def quarters(value, places):
+        return [value[i * half : (i + 1) * half, j * half : (j + 1) * half] for i, j in places]
+
+    upper_places = ((0, 0), (0, 1), (1, 1))
+    every_place = ((0, 0), (0, 1), (1, 0), (1, 1))
+    tiles = quarters(gram_one, upper_places) + quarters(cross_sum, every_place) + quarters(gram_two, upper_places)
+    for at, tile in enumerate(tiles):
+        packed[pl.ds(at * half, half), :] = tile
+
+    share = fold.shape[0]
+    slice_rows = share // CHIPS
+    base = core * share
+
+    def sum_copy(stage, source, target):
+        return remote(source, target, sum_sem, (stage,), partner)
+
+    fold_copy = sum_copy(0, packed.at[pl.ds((1 - core) * share, share)], fold_in)
+    fold_copy.start()
+
+    tile_count = owner.shape[0]
+    tile_rows = span // tile_count
+    inv_two_t = part_two_t - exact(above[...].T, inv_one_t, ((1,), (0,))) * two_row
+    inverse_one[...] = inv_one_t.T
+    inv_two = inv_two_t.T
+
+    def chip_at(offset):
+        flat = lax.rem(chip + offset, CHIPS)
+        return flat, device(flat // 4, lax.rem(flat // 2, 2), lax.rem(flat, 2), core)
+
+    fold_copy.wait_recv()
+    fold[...] = packed[pl.ds(base, share), :] + fold_in[...]
+    order = sorted(range(1, CHIPS), key=lambda offset: -min(offset, CHIPS - offset))
+    chip_copies = []
+    for offset in order:
+        flat, peer = chip_at(offset)
+        copy = remote(
+            fold.at[pl.ds(flat * slice_rows, slice_rows)], part_in.at[offset - 1], chip_sem, (offset - 1,), peer
+        )
+        copy.start()
+        chip_copies.append(copy)
+
+    names = [owner[at] for at in range(tile_count)]
+    ranks = [sum([jnp.where(names[before] == names[at], 1, 0) for before in range(at)], jnp.int32(0)) for at in range(tile_count)]
+
+    def slot_value(name, rank):
+        value = jnp.zeros((tile_rows, width), jnp.float32)
+        for at in range(tile_count):
+            chosen = (names[at] == name) & (ranks[at] == rank)
+            value = jnp.where(chosen, inv_two[at * tile_rows : (at + 1) * tile_rows], value)
+        return value
+
+    tile_copies = []
+    for offset in range(1, COLS):
+        name = lax.rem(col + offset, COLS)
+        for rank in range(CAP):
+            outgoing[offset - 1, rank] = slot_value(name, rank)
+        copy = remote(
+            outgoing.at[offset - 1], delivered.at[pl.ds(col * CAP, CAP)], tile_sem, (offset - 1,), (row, name)
+        )
+        copy.start()
+        tile_copies.append(copy)
+    for rank in range(CAP):
+        delivered[col * CAP + rank] = slot_value(col, rank)
+
+    for copy in chip_copies:
+        copy.wait_recv()
+    value = fold[pl.ds(chip * slice_rows, slice_rows), :]
+    for slot in range(CHIPS - 1):
+        value = value + part_in[slot]
+    mine_rows = pl.ds(base + chip * slice_rows, slice_rows)
+    full[mine_rows, :] = value
+    spread_copies = []
+    for offset in order:
+        _, peer = chip_at(offset)
+        copy = remote(full.at[mine_rows], full.at[mine_rows], spread_sem, (offset - 1,), peer)
+        copy.start()
+        spread_copies.append(copy)
+    for copy in spread_copies:
+        copy.wait_recv()
+    half_rows = pl.ds(base, share)
+    last_copy = sum_copy(1, full.at[half_rows], full.at[half_rows])
+    last_copy.start()
+    last_copy.wait_recv()
+
+    def tile_at(at):
+        return full[pl.ds(at * half, half), :]
+
+    def square(first, second, third, fourth):
+        return jnp.concatenate(
+            [jnp.concatenate([first, second], axis=1), jnp.concatenate([third, fourth], axis=1)], axis=0
+        )
+
+    pa = above[...]
+    pa_t = pa.T
+    plain = ((1,), (0,))
+    diag_one_value = diag_one[...] - square(tile_at(0), tile_at(1), tile_at(1).T, tile_at(2))
+    cross_total = square(tile_at(3), tile_at(4), tile_at(5), tile_at(6))
+    diag_one[...] = diag_one_value
+    cross_value = -(cross_total + exact(diag_one_value, pa, plain))
+    cross_two[...] = cross_value
+    gram_total = square(tile_at(7), tile_at(8), tile_at(8).T, tile_at(9)) - exact(cross_total.T, pa, plain)
+    diag_two[...] = (diag_two[...] - gram_total) - exact(pa_t, cross_value, plain)
+
+    for copy in tile_copies:
+        copy.wait_recv()
+    pl.when(jnp.logical_not(stays))(lambda: moved.wait_send())
+    for copy in chip_copies + spread_copies + tile_copies + [fold_copy, last_copy]:
+        copy.wait_send()
+    for at in range(CHUNKS):
+        for copy in (near_copy(at), far_copy(at), relay_copy(at)):
+            copy.wait_send()
+        for step in range(4):
+            pair_copy(at, step).wait_send()
+        for slot, peer in enumerate((near, away, near)):
+            major_copy(at, slot, peer).wait_send()
+
+
+def fused(matrix, panel_one, panel_two, struct_one, struct_two, lower_one, above, lower_two, tile_owner):
+    depth, _ = matrix.shape
+    span, width = panel_one.shape
+    chunk = 2 * width // CHUNKS
+    tile_count = tile_owner.shape[0]
+    share = 5 * (width // 2)
+    mask_rows = -(-(COLS + 1) * (span // LANES) // 8) * 8
+    dma = pltpu.SemaphoreType.DMA
+    vmem = lambda *shape: pltpu.VMEM(shape, jnp.float32)
+    half_vmem = lambda *shape: pltpu.VMEM(shape, jnp.bfloat16)
+    anywhere = pl.BlockSpec(memory_space=pl.ANY)
+    whole = pl.BlockSpec(memory_space=pltpu.VMEM)
+    scalars = pl.BlockSpec(memory_space=pltpu.SMEM)
+    shape = lambda *dims: jax.ShapeDtypeStruct(dims, jnp.float32)
+    return tuple(pl.pallas_call(
+        fused_kernel,
+        out_shape=[
+            shape(span, width),
+            shape(width, width),
+            shape(width, width),
+            shape(width, width),
+            shape(COLS * CAP, span // tile_count, width),
+        ],
+        in_specs=[anywhere] * 3 + [whole] * 5 + [scalars],
+        out_specs=[whole] * 5,
+        scratch_shapes=[
+            vmem(2, depth, span),
+            half_vmem(8, depth, span),
+            half_vmem(8, depth, span),
+            vmem(2, span, width),
+            vmem(COLS, CHUNKS, span, chunk),
+            half_vmem(CHUNKS, 2 * chunk, depth),
+            vmem(CHUNKS, 4, chunk, span),
+            vmem(CHUNKS, 4, chunk, span),
+            vmem(CHUNKS, 4, chunk, span),
+            vmem(CHUNKS, 3, chunk, span),
+            vmem(2, mask_rows, LANES),
+            vmem(2, span, width),
+            vmem(CHUNKS, chunk, span),
+            vmem(2 * share, LANES),
+            vmem(share, LANES),
+            vmem(share, LANES),
+            vmem(CHIPS - 1, share // CHIPS, LANES),
+            vmem(2 * share, LANES),
+            vmem(COLS - 1, CAP, span // tile_count, width),
+            dma((2,)),
+            dma((2,)),
+            dma((2,)),
+            dma((2, CHUNKS)),
+            dma((2, CHUNKS)),
+            dma((2, CHUNKS)),
+            dma((2, CHUNKS, 4)),
+            dma((2, CHUNKS, 3)),
+            dma((2, 2)),
+            dma((2, CHIPS - 1)),
+            dma((2, CHIPS - 1)),
+            dma((2, COLS - 1)),
+        ],
+        compiler_params=pltpu.CompilerParams(
+            collective_id=3, has_side_effects=True, vmem_limit_bytes=62 * 2**20
+        ),
+        cost_estimate=pl.CostEstimate(
+            flops=12 * matrix.size * width, bytes_accessed=4 * matrix.size, transcendentals=0
+        ),
+    )(
+        matrix,
+        panel_one,
+        panel_two,
+        struct_one.reshape(-1, LANES),
+        struct_two.reshape(-1, LANES),
+        lower_one,
+        above,
+        lower_two,
+        tile_owner.reshape(-1),
+    ))
+
+
 def local(
     ancestor_inverse,
     panel_one,
@@ -466,6 +694,18 @@
     row_index = lax.axis_index("row")
     col_index = lax.axis_index("col")
     local_rows = panel_one.shape[0]
+    if fits_fused(ancestor_inverse, panel_one, struct_one, struct_two, tile_owner, row_count, col_count):
+        return fused(
+            ancestor_inverse,
+            panel_one,
+            panel_two,
+            struct_one,
+            struct_two,
+            lower_one,
+            panel_above,
+            lower_two,
+            tile_owner,
+        )
     order = local_rows * row_count * col_count
     width = panel_one.shape[1]
     mask_one = row_mask(struct_one, order)
@@ -478,16 +718,10 @@
     result_mask_two = lax.dynamic_slice_in_dim(mask_two, result_start, local_rows)[:, None]
 
     both = jnp.concatenate([local_one, local_two], axis=1)
-    late = both
-    if local_rows % 128 == 0 and row_count // 2 == 4:
-        high, low = gather_columns(both.T, col_count)
-        high, late = lax.optimization_barrier((high, both))
-        product = product_rows(ancestor_inverse, high, low, row_count).T
-    else:
-        gathered = lax.all_gather(both, "col", axis=0, tiled=True)
-        product = scatter_rows(contract_rows(ancestor_inverse, gathered, lax.Precision.HIGH), row_count)
+    gathered = lax.all_gather(both, "col", axis=0, tiled=True)
+    product = scatter_rows(contract_rows(ancestor_inverse, gathered, lax.Precision.HIGH), row_count)
     moves = [(f, (f % row_count) * col_count + f // row_count) for f in range(row_count * col_count)]
-    resident = lax.ppermute(late, ("row", "col"), moves)
+    resident = lax.ppermute(both, ("row", "col"), moves)
     resident_one = resident[:, :width]
     resident_two = resident[:, width:]
     inverse_one = -product[:, :width] * result_mask_one

time: 202 us -> 184 us (0.911)
  matrix products: 9.08 us -> 0 us
  waiting for transfers between devices: 7.69 us -> 0 us
  local copies, waits for them, and re-layouts: 3.29 us -> 8.64 us
  starting transfers between devices: 4.36 us -> 0 us
  other arithmetic: 2.4 us -> 0 us
    dot_general x11 -> x0, matrix products: 9.08 us -> none  [the longest x5 3.51 us: matmul(): jnp.dot(left, right, precision=lax.Precision.HIGHEST, preferred_element_t...]
    all_to_all x1 -> x0, waiting for transfers between devices: 7.68 us -> none  [deliver(): lax.all_to_all(outgoing, 'col', split_axis=0, concat_axis=0, tiled=True)]
    unnamed x23 -> x5, local copies, waits for them, and re-layouts: 1.81 us -> 8.64 us
    all_to_all x1 -> x0, starting transfers between devices: 3.65 us -> none  [deliver(): lax.all_to_all(outgoing, 'col', split_axis=0, concat_axis=0, tiled=True)]
    pallas_call x3 -> x1, Pallas kernels: 174 us -> 173 us  [fused(): pl.pallas_call(fused_kernel, out_shape=[shape(span, width), shape(width,...]
  transfers between devices with their start and end apart: 2 -> 0, of which waited for: 1 -> 0; matrix products, arithmetic and copies ran while one was open for 2% -> 0% of each run, Pallas kernels for 60% -> 0%
where the time goes in v1:
time: 184 us; the launch traced here: 182 us
  Pallas kernels  173 us (94%)
  local copies, waits for them, and re-layouts  8.64 us (5%)
    pallas_call x1, Pallas kernels, fused(): pl.pallas_call(fused_kernel, out_shape=[shape(span, width), shape(width,...  173 us
    unnamed x5, local copies, waits for them, and re-layouts  8.64 us

profile of v1, /device:TPU:0, one launch (start us, length us, event | category | flops | bytes accessed | tf_op | source)
XLA Modules:
  0.0 182.2 jit_solution(16038158388635324179)
XLA Ops:
  0.6 172.9 %shard_map.128 = (f32[384,256]{1,0:T(8,128)}, f32[256,256]{1,0:T(8,128)}, f32[256,256]{1,0:T(8,128)}, f32[256,256]{1,0:T(8,128)}, f32[8,64,256]{2,1,0:T(8,128)}) custom-call(f32[1536,3072]{1,0:T(8,128)} %matrix.1, f32[384,256]{1,0:T(8,128)} %panel_one.1, f32[384,256]{1,0:T(8,128)} %panel_two.1, s32[84,128]{1,0:T(8,128)} %bitcast.3, s32[72,128]{1,0:T(8,128)} %bitcast.4, ...), custom_call_target="tpu_custom_call" | custom-call | flops 14495514624 | bytes 18874368 | tf_op jit(solution)/shard_map/pallas_call | solution.py:618
  173.5 1.8 copy.19
  175.3 1.7 copy.20
  177.0 1.7 copy.21
  178.6 1.7 copy.22
  180.3 1.9 %copy.23 = f32[8,64,256]{2,1,0:T(8,128)} copy(f32[8,64,256]{2,1,0:T(8,128)} %get-tuple-element.14) | data formatting | bytes 1048576

commit v2 on v1

--- a/solution.py
+++ b/solution.py
@@ -266,11 +266,12 @@
 
 
 def fused_kernel(
-    matrix, panel_one, panel_two, struct_one, struct_two, lower_one, above, lower_two, owner,
-    inverse_one, diag_one, cross_two, diag_two, delivered,
-    window, high, low, own, land, left, other, mine, pair_in, major_in, masks, resident, product,
-    packed, fold_in, fold, part_in, full, outgoing,
-    fetch_sem, own_sem, move_sem, near_gather, far_gather, relay_gather, pair_sem, major_sem, sum_sem, chip_sem,
+    matrix, panel_one, panel_two, struct_one_in, struct_two_in, lower_one_in, above_in, lower_two_in, owner,
+    inverse_one_out, diag_one_out, cross_two_out, diag_two_out, delivered,
+    inverse_one, diag_one, cross_two, diag_two, tiles_here,
+    struct_one, struct_two, lower_one, above, lower_two, window, high, low, own, land, left, other, mine, pair_in, major_in, masks, turned, resident, product,
+    inv_one_t, part_two_t, panel_two_t, correction, packed, fold_in, fold, part_in, full, outgoing,
+    out_sem, small_sem, fetch_sem, own_sem, turn_sem, move_sem, near_gather, far_gather, relay_gather, pair_sem, major_sem, sum_sem, chip_sem,
     spread_sem, tile_sem,
 ):
     row = lax.axis_index("row")
@@ -317,6 +318,18 @@
             matrix.at[:, pl.ds(pl.multiple_of(target * span, LANES), span)], window.at[which], fetch_sem.at[which]
         )
 
+    small_pairs = (
+        (struct_one_in, struct_one),
+        (struct_two_in, struct_two),
+        (lower_one_in, lower_one),
+        (above_in, above),
+        (lower_two_in, lower_two),
+    )
+    small_copies = [
+        pltpu.make_async_copy(source, target, small_sem.at[at]) for at, (source, target) in enumerate(small_pairs)
+    ]
+    for copy in small_copies:
+        copy.start()
     barrier = pltpu.get_barrier_semaphore()
     devices = ROWS * COLS
     for offset in range(1, devices):
@@ -341,20 +354,68 @@
         slot = (1 - x) * 2 + core
         return remote(land.at[slot, at], land.at[slot, at], relay_gather, (at,), partner)
 
-    place = row * COLS + col
-    move_row, move_col = lax.rem(place, ROWS), place // ROWS
-    stays = (move_row == row) & (move_col == col)
-    moved = remote(own, resident, move_sem, (), (move_row, move_col))
-    kept = pltpu.make_async_copy(own, resident, move_sem.at[1])
+    turns = core != y
+    direct = jnp.where(x == upper, 0, 1)
+    relays_move = lower == x
+
+    def move_copy(source, slot, panel, at, peer):
+        return pltpu.make_async_remote_copy(
+            src_ref=source.at[panel],
+            dst_ref=resident.at[slot, panel],
+            send_sem=move_sem.at[0, panel, at],
+            recv_sem=move_sem.at[1, panel, slot],
+            device_id=peer,
+            device_id_type=MESH,
+        )
+
+    def climb(source, panel, at, from_y):
+        peer = device(2 * from_y + x, y, x, lower)
+        return move_copy(source, direct, panel, at, peer), (peer[0] == row) & (peer[1] == col)
+
+    def start_climb(source, panel, at, from_y):
+        copy, stays = climb(source, panel, at, from_y)
+        kept = pltpu.make_async_copy(source.at[panel], resident.at[direct, panel], move_sem.at[1, panel, direct])
+        pl.when(stays)(lambda: kept.start())
+        pl.when(jnp.logical_not(stays))(lambda: copy.start())
+
+    def end_climb(source, panel, at, from_y):
+        copy, stays = climb(source, panel, at, from_y)
+        pl.when(jnp.logical_not(stays))(lambda: copy.wait_send())
+
+    turn = [remote(own.at[panel], turned.at[panel], turn_sem, (panel,), beside) for panel in range(2)]
+    passed = [move_copy(resident.at[1], 0, panel, 2, across) for panel in range(2)]
+
+    def climb_turned(panel):
+        @pl.when(jnp.logical_not(turns))
+        def _():
+            turn[panel].wait_recv()
+            start_climb(turned, panel, 1, 1 - y)
+
+    def pass_on(panel):
+        @pl.when(relays_move)
+        def _():
+            move_copy(own, 1, panel, 0, beside).wait_recv()
+            passed[panel].start()
+
     for at in range(CHUNKS):
         far_copy(at, piece(at)).start()
         near_copy(at, piece(at)).start()
         if at == 0:
-            pl.when(stays)(lambda: kept.start())
-            pl.when(jnp.logical_not(stays))(lambda: moved.start())
+            @pl.when(turns)
+            def _():
+                for copy in turn:
+                    copy.start()
+
+            @pl.when(jnp.logical_not(turns))
+            def _():
+                for panel in range(2):
+                    start_climb(own, panel, 0, y)
+
     for at in range(CHUNKS):
         land[col, at] = piece(at)[...]
 
+    for copy in small_copies:
+        copy.wait()
     blocks = span // LANES
     slots_of = COLS * blocks
     mask_rows = masks.shape[1]
@@ -428,6 +489,7 @@
                 fetch(step + 1, which).start()
 
             multiply(0, step, which)
+        pl.when(step == 1)(lambda: climb_turned(1))
         return carry
 
     def later_steps(at):
@@ -441,156 +503,248 @@
     def major_copy(at, slot, peer):
         return remote(mine.at[at, slot], major_in.at[at, slot], major_sem, (at, slot), peer)
 
-    def collect(at):
+    def open_near(at):
         pair_copy(at, 0).wait_recv()
         mine[at, 0] = mine[at, 0] + pair_in[at, 0]
         major_copy(at, 0, near).start()
+
+    def open_away(at):
         pair_copy(at, 1).wait_recv()
         mine[at, 1] = mine[at, 1] + pair_in[at, 1]
         major_copy(at, 0, near).wait_recv()
         mine[at, 1] = mine[at, 1] + major_in[at, 0]
         major_copy(at, 1, away).start()
+
+    def close_near(at):
         pair_copy(at, 2).wait_recv()
         mine[at, 2] = mine[at, 2] + pair_in[at, 2]
         major_copy(at, 2, near).start()
+
+    def collect(at):
         pair_copy(at, 3).wait_recv()
         value = mine[at, 3] + pair_in[at, 3]
         major_copy(at, 1, away).wait_recv()
         major_copy(at, 2, near).wait_recv()
         product[at] = value + (major_in[at, 1] + major_in[at, 2])
 
-    prepare(0)
-    lax.fori_loop(0, 4, first_step, 0)
-
-    def rest_of(at, carry):
-        prepare(at)
-        later_steps(at)
-        collect(at - 1)
-        return carry
-
-    lax.fori_loop(1, CHUNKS, rest_of, 0)
-    collect(CHUNKS - 1)
-
-    one_row = mask_of(0, slots_of)
-    two_row = mask_of(1, slots_of)
-    inv_one_t = -(jnp.concatenate([product[at] for at in range(per_panel)], axis=0) * one_row)
-    part_two_t = -(jnp.concatenate([product[at] for at in range(per_panel, CHUNKS)], axis=0) * two_row)
-    moved.wait_recv()
-    last = ((1,), (1,))
-    panel_one_t = resident[0].T
-    panel_two_t = resident[1].T
-    gram_one = exact(panel_one_t, inv_one_t, last)
-    cross_sum = exact(inv_one_t * two_row, panel_two_t, last)
-    gram_two = exact(panel_two_t, part_two_t, last)
     half = width // 2
-
-    def quarters(value, places):
-        return [value[i * half : (i + 1) * half, j * half : (j + 1) * half] for i, j in places]
-
-    upper_places = ((0, 0), (0, 1), (1, 1))
-    every_place = ((0, 0), (0, 1), (1, 0), (1, 1))
-    tiles = quarters(gram_one, upper_places) + quarters(cross_sum, every_place) + quarters(gram_two, upper_places)
-    for at, tile in enumerate(tiles):
-        packed[pl.ds(at * half, half), :] = tile
-
-    share = fold.shape[0]
-    slice_rows = share // CHIPS
-    base = core * share
-
-    def sum_copy(stage, source, target):
-        return remote(source, target, sum_sem, (stage,), partner)
-
-    fold_copy = sum_copy(0, packed.at[pl.ds((1 - core) * share, share)], fold_in)
-    fold_copy.start()
-
-    tile_count = owner.shape[0]
-    tile_rows = span // tile_count
-    inv_two_t = part_two_t - exact(above[...].T, inv_one_t, ((1,), (0,))) * two_row
-    inverse_one[...] = inv_one_t.T
-    inv_two = inv_two_t.T
+    share_of = (4 * half, 2 * half)
+    starts = (0, 4 * half)
+    order = sorted(range(1, CHIPS), key=lambda offset: -min(offset, CHIPS - offset))
+    plain, last = ((1,), (0,)), ((1,), (1,))
 
     def chip_at(offset):
         flat = lax.rem(chip + offset, CHIPS)
         return flat, device(flat // 4, lax.rem(flat // 2, 2), lax.rem(flat, 2), core)
 
-    fold_copy.wait_recv()
-    fold[...] = packed[pl.ds(base, share), :] + fold_in[...]
-    order = sorted(range(1, CHIPS), key=lambda offset: -min(offset, CHIPS - offset))
-    chip_copies = []
-    for offset in order:
-        flat, peer = chip_at(offset)
-        copy = remote(
-            fold.at[pl.ds(flat * slice_rows, slice_rows)], part_in.at[offset - 1], chip_sem, (offset - 1,), peer
-        )
+    class Total:
+        def __init__(self, at):
+            self.at, self.share, self.start = at, share_of[at], starts[at]
+            self.rows = self.share // CHIPS
+            self.base = 2 * self.start + core * self.share
+            self.half_rows = pl.ds(self.base, self.share)
+            self.sent = []
+
+        def partner_copy(self, stage, source, target):
+            copy = remote(source, target, sum_sem, (self.at, stage), partner)
+            self.sent.append(copy)
+            copy.start()
+            return copy
+
+        def begin(self, tiles):
+            for at in range(2 * self.share // half):
+                tile = tiles[at] if at < len(tiles) else jnp.zeros((half, half), jnp.float32)
+                packed[pl.ds(2 * self.start + at * half, half), :] = tile
+            theirs = pl.ds(2 * self.start + (1 - core) * self.share, self.share)
+            self.first = self.partner_copy(0, packed.at[theirs], fold_in.at[pl.ds(self.start, self.share)])
+
+        def scatter(self):
+            self.first.wait_recv()
+            rows = pl.ds(self.start, self.share)
+            fold[rows, :] = packed[self.half_rows, :] + fold_in[rows, :]
+            self.copies = []
+            for offset in order:
+                flat, peer = chip_at(offset)
+                copy = remote(
+                    fold.at[pl.ds(self.start + flat * self.rows, self.rows)],
+                    part_in.at[offset - 1, pl.ds(self.start // CHIPS, self.rows)],
+                    chip_sem,
+                    (self.at, offset - 1),
+                    peer,
+                )
+                copy.start()
+                self.copies.append(copy)
+
+        def gather(self):
+            for copy in self.copies:
+                copy.wait_recv()
+            value = fold[pl.ds(self.start + chip * self.rows, self.rows), :]
+            for slot in range(CHIPS - 1):
+                value = value + part_in[slot, pl.ds(self.start // CHIPS, self.rows), :]
+            mine_rows = pl.ds(self.base + chip * self.rows, self.rows)
+            full[mine_rows, :] = value
+            self.sent += self.copies
+            self.copies = []
+            for offset in order:
+                copy = remote(
+                    full.at[mine_rows], full.at[mine_rows], spread_sem, (self.at, offset - 1), chip_at(offset)[1]
+                )
+                copy.start()
+                self.copies.append(copy)
+
+        def finish(self):
+            for copy in self.copies:
+                copy.wait_recv()
+            self.final = self.partner_copy(1, full.at[self.half_rows], full.at[self.half_rows])
+            self.sent += self.copies
+
+        def tile(self, at):
+            return full[pl.ds(2 * self.start + at * half, half), :]
+
+    def quarters(value, places):
+        return [value[i * half : (i + 1) * half, j * half : (j + 1) * half] for i, j in places]
+
+    upper_places = ((0, 0), (0, 1), (1, 1))
+    every_place = ((0, 0), (0, 1), (1, 0), (1, 1))
+    tile_count = owner.shape[0]
+    tile_rows = span // tile_count
+    names = [owner[at] for at in range(tile_count)]
+    ranks = [
+        sum([jnp.where(names[before] == names[at], 1, 0) for before in range(at)], jnp.int32(0))
+        for at in range(tile_count)
+    ]
+    tile_copies = []
+
+    def send_tiles(part, values):
+        columns = pl.ds(part * half, half)
+
+        def slot_value(name, rank):
+            value = jnp.zeros((tile_rows, half), jnp.float32)
+            for at in range(tile_count):
+                chosen = (names[at] == name) & (ranks[at] == rank)
+                value = jnp.where(chosen, values[at * tile_rows : (at + 1) * tile_rows], value)
+            return value
+
+        for offset in range(1, COLS):
+            name = lax.rem(col + offset, COLS)
+            for rank in range(CAP):
+                outgoing[offset - 1, rank, :, columns] = slot_value(name, rank)
+            copy = remote(
+                outgoing.at[offset - 1, :, :, columns],
+                delivered.at[pl.ds(col * CAP, CAP), :, columns],
+                tile_sem,
+                (part, offset - 1),
+                (row, name),
+            )
+            copy.start()
+            tile_copies.append(copy)
+        for rank in range(CAP):
+            tiles_here[rank, :, columns] = slot_value(col, rank)
+
+    first_total, second_total = Total(0), Total(1)
+
+    prepare(0)
+    climb_turned(0)
+    lax.fori_loop(0, 4, first_step, 0)
+    prepare(1)
+    open_near(0)
+    later_steps(1)
+    close_near(0)
+    pass_on(0)
+    prepare(2)
+    later_steps(2)
+    open_near(1)
+    open_away(0)
+    pass_on(1)
+    close_near(1)
+    open_away(1)
+    collect(0)
+    prepare(3)
+    open_near(2)
+    later_steps(3)
+    collect(1)
+    one_row = mask_of(0, slots_of)
+    two_row = mask_of(1, slots_of)
+    inv_one_t[...] = -(jnp.concatenate([product[at] for at in range(per_panel)], axis=0) * one_row)
+    for copy in passed:
+        copy.wait_recv()
+    panel_two_t[...] = resident[0, 1].T
+    gram_one = exact(resident[0, 0].T, inv_one_t[...], last)
+    cross_sum = exact(inv_one_t[...] * two_row, panel_two_t[...], last)
+    first_total.begin(quarters(gram_one, upper_places) + quarters(cross_sum, every_place))
+    above_t = above[...].T
+    correction[...] = exact(above_t, inv_one_t[...], plain) * two_row
+    inverse_one[...] = inv_one_t[...].T
+    outs = [pltpu.make_async_copy(inverse_one, inverse_one_out, out_sem.at[0])]
+    outs[0].start()
+    first_total.scatter()
+    open_away(2)
+    close_near(2)
+    open_near(3)
+    collect(2)
+    part_two_t[pl.ds(0, half), :] = -(product[2] * two_row)
+    send_tiles(0, (part_two_t[pl.ds(0, half), :] - correction[pl.ds(0, half), :]).T)
+    open_away(3)
+    close_near(3)
+    first_total.gather()
+    collect(3)
+    part_two_t[pl.ds(half, half), :] = -(product[3] * two_row)
+    gram_two = exact(panel_two_t[...], part_two_t[...], last)
+    second_total.begin(quarters(gram_two, upper_places))
+    first_total.finish()
+    second_total.scatter()
+    send_tiles(1, (part_two_t[pl.ds(half, half), :] - correction[pl.ds(half, half), :]).T)
+
+    here = pltpu.make_async_copy(tiles_here, delivered.at[pl.ds(col * CAP, CAP)], out_sem.at[4])
+    here.start()
+    outs.append(here)
+
+    def put(at, source, target):
+        copy = pltpu.make_async_copy(source, target, out_sem.at[at])
         copy.start()
-        chip_copies.append(copy)
-
-    names = [owner[at] for at in range(tile_count)]
-    ranks = [sum([jnp.where(names[before] == names[at], 1, 0) for before in range(at)], jnp.int32(0)) for at in range(tile_count)]
-
-    def slot_value(name, rank):
-        value = jnp.zeros((tile_rows, width), jnp.float32)
-        for at in range(tile_count):
-            chosen = (names[at] == name) & (ranks[at] == rank)
-            value = jnp.where(chosen, inv_two[at * tile_rows : (at + 1) * tile_rows], value)
-        return value
-
-    tile_copies = []
-    for offset in range(1, COLS):
-        name = lax.rem(col + offset, COLS)
-        for rank in range(CAP):
-            outgoing[offset - 1, rank] = slot_value(name, rank)
-        copy = remote(
-            outgoing.at[offset - 1], delivered.at[pl.ds(col * CAP, CAP)], tile_sem, (offset - 1,), (row, name)
-        )
-        copy.start()
-        tile_copies.append(copy)
-    for rank in range(CAP):
-        delivered[col * CAP + rank] = slot_value(col, rank)
-
-    for copy in chip_copies:
-        copy.wait_recv()
-    value = fold[pl.ds(chip * slice_rows, slice_rows), :]
-    for slot in range(CHIPS - 1):
-        value = value + part_in[slot]
-    mine_rows = pl.ds(base + chip * slice_rows, slice_rows)
-    full[mine_rows, :] = value
-    spread_copies = []
-    for offset in order:
-        _, peer = chip_at(offset)
-        copy = remote(full.at[mine_rows], full.at[mine_rows], spread_sem, (offset - 1,), peer)
-        copy.start()
-        spread_copies.append(copy)
-    for copy in spread_copies:
-        copy.wait_recv()
-    half_rows = pl.ds(base, share)
-    last_copy = sum_copy(1, full.at[half_rows], full.at[half_rows])
-    last_copy.start()
-    last_copy.wait_recv()
-
-    def tile_at(at):
-        return full[pl.ds(at * half, half), :]
+        outs.append(copy)
 
     def square(first, second, third, fourth):
         return jnp.concatenate(
             [jnp.concatenate([first, second], axis=1), jnp.concatenate([third, fourth], axis=1)], axis=0
         )
 
-    pa = above[...]
-    pa_t = pa.T
-    plain = ((1,), (0,))
-    diag_one_value = diag_one[...] - square(tile_at(0), tile_at(1), tile_at(1).T, tile_at(2))
-    cross_total = square(tile_at(3), tile_at(4), tile_at(5), tile_at(6))
+    first_total.final.wait_recv()
+    tile = first_total.tile
+    diag_one_value = diag_one[...] - square(tile(0), tile(1), tile(1).T, tile(2))
+    cross_total = square(tile(3), tile(4), tile(5), tile(6))
     diag_one[...] = diag_one_value
-    cross_value = -(cross_total + exact(diag_one_value, pa, plain))
+    put(1, diag_one, diag_one_out)
+    cross_value = -(cross_total + exact(diag_one_value, above[...], plain))
     cross_two[...] = cross_value
-    gram_total = square(tile_at(7), tile_at(8), tile_at(8).T, tile_at(9)) - exact(cross_total.T, pa, plain)
-    diag_two[...] = (diag_two[...] - gram_total) - exact(pa_t, cross_value, plain)
+    put(2, cross_two, cross_two_out)
+    diag_two[...] = diag_two[...] + (exact(cross_total.T, above[...], plain) - exact(above_t, cross_value, plain))
+    second_total.gather()
+    second_total.finish()
+    second_total.final.wait_recv()
+    tile = second_total.tile
+    diag_two[...] = diag_two[...] - square(tile(0), tile(1), tile(1).T, tile(2))
+    put(3, diag_two, diag_two_out)
 
     for copy in tile_copies:
         copy.wait_recv()
-    pl.when(jnp.logical_not(stays))(lambda: moved.wait_send())
-    for copy in chip_copies + spread_copies + tile_copies + [fold_copy, last_copy]:
+
+    for panel in range(2):
+
+        @pl.when(turns)
+        def _():
+            turn[panel].wait_send()
+
+        @pl.when(jnp.logical_not(turns))
+        def _():
+            end_climb(own, panel, 0, y)
+            end_climb(turned, panel, 1, 1 - y)
+
+        pl.when(relays_move)(lambda: passed[panel].wait_send())
+
+    for copy in outs:
+        copy.wait()
+    for copy in first_total.sent + second_total.sent + tile_copies:
         copy.wait_send()
     for at in range(CHUNKS):
         for copy in (near_copy(at), far_copy(at), relay_copy(at)):
@@ -601,21 +755,33 @@
             major_copy(at, slot, peer).wait_send()
 
 
+def place_kernel(count, *refs):
+    sources, targets, buffers, sems = refs[:count], refs[count : 2 * count], refs[2 * count : -1], refs[-1]
+    loads = [pltpu.make_async_copy(sources[at], buffers[at], sems.at[0, at]) for at in range(count)]
+    stores = [pltpu.make_async_copy(buffers[at], targets[at], sems.at[1, at]) for at in range(count)]
+    for copy in loads:
+        copy.start()
+    for load, store in zip(loads, stores):
+        load.wait()
+        store.start()
+    for copy in stores:
+        copy.wait()
+
+
 def fused(matrix, panel_one, panel_two, struct_one, struct_two, lower_one, above, lower_two, tile_owner):
     depth, _ = matrix.shape
     span, width = panel_one.shape
     chunk = 2 * width // CHUNKS
     tile_count = tile_owner.shape[0]
-    share = 5 * (width // 2)
+    share = 6 * (width // 2)
     mask_rows = -(-(COLS + 1) * (span // LANES) // 8) * 8
     dma = pltpu.SemaphoreType.DMA
     vmem = lambda *shape: pltpu.VMEM(shape, jnp.float32)
     half_vmem = lambda *shape: pltpu.VMEM(shape, jnp.bfloat16)
     anywhere = pl.BlockSpec(memory_space=pl.ANY)
-    whole = pl.BlockSpec(memory_space=pltpu.VMEM)
     scalars = pl.BlockSpec(memory_space=pltpu.SMEM)
     shape = lambda *dims: jax.ShapeDtypeStruct(dims, jnp.float32)
-    return tuple(pl.pallas_call(
+    results = pl.pallas_call(
         fused_kernel,
         out_shape=[
             shape(span, width),
@@ -624,9 +790,19 @@
             shape(width, width),
             shape(COLS * CAP, span // tile_count, width),
         ],
-        in_specs=[anywhere] * 3 + [whole] * 5 + [scalars],
-        out_specs=[whole] * 5,
+        in_specs=[anywhere] * 8 + [scalars],
+        out_specs=[anywhere] * 5,
         scratch_shapes=[
+            vmem(span, width),
+            vmem(width, width),
+            vmem(width, width),
+            vmem(width, width),
+            vmem(CAP, span // tile_count, width),
+            pltpu.VMEM((struct_one.shape[0] // LANES, LANES), jnp.int32),
+            pltpu.VMEM((struct_two.shape[0] // LANES, LANES), jnp.int32),
+            vmem(width, width),
+            vmem(width, width),
+            vmem(width, width),
             vmem(2, depth, span),
             half_vmem(8, depth, span),
             half_vmem(8, depth, span),
@@ -639,28 +815,36 @@
             vmem(CHUNKS, 3, chunk, span),
             vmem(2, mask_rows, LANES),
             vmem(2, span, width),
+            vmem(2, 2, span, width),
             vmem(CHUNKS, chunk, span),
+            vmem(width, span),
+            vmem(width, span),
+            vmem(width, span),
+            vmem(width, span),
             vmem(2 * share, LANES),
             vmem(share, LANES),
             vmem(share, LANES),
             vmem(CHIPS - 1, share // CHIPS, LANES),
             vmem(2 * share, LANES),
             vmem(COLS - 1, CAP, span // tile_count, width),
+            dma((5,)),
+            dma((5,)),
             dma((2,)),
             dma((2,)),
-            dma((2,)),
+            dma((2, 2)),
+            dma((2, 2, 3)),
             dma((2, CHUNKS)),
             dma((2, CHUNKS)),
             dma((2, CHUNKS)),
             dma((2, CHUNKS, 4)),
             dma((2, CHUNKS, 3)),
-            dma((2, 2)),
-            dma((2, CHIPS - 1)),
-            dma((2, CHIPS - 1)),
-            dma((2, COLS - 1)),
+            dma((2, 2, 2)),
+            dma((2, 2, CHIPS - 1)),
+            dma((2, 2, CHIPS - 1)),
+            dma((2, 2, COLS - 1)),
         ],
         compiler_params=pltpu.CompilerParams(
-            collective_id=3, has_side_effects=True, vmem_limit_bytes=62 * 2**20
+            collective_id=3, has_side_effects=True, vmem_limit_bytes=54 * 2**20
         ),
         cost_estimate=pl.CostEstimate(
             flops=12 * matrix.size * width, bytes_accessed=4 * matrix.size, transcendentals=0
@@ -675,7 +859,15 @@
         above,
         lower_two,
         tile_owner.reshape(-1),
-    ))
+    )
+    return tuple(pl.pallas_call(
+        functools.partial(place_kernel, len(results)),
+        out_shape=[shape(*result.shape) for result in results],
+        in_specs=[anywhere] * len(results),
+        out_specs=[anywhere] * len(results),
+        scratch_shapes=[vmem(*result.shape) for result in results] + [dma((2, len(results)))],
+        compiler_params=pltpu.CompilerParams(vmem_limit_bytes=60 * 2**20),
+    )(*results))
 
 
 def local(

time: 184 us -> 128 us (0.70)
  Pallas kernels: 173 us -> 127 us
  local copies, waits for them, and re-layouts: 8.64 us -> 0 us
    pallas_call x1, Pallas kernels: 173 us -> 124 us  [fused(): pl.pallas_call(fused_kernel, out_shape=[shape(span, width), shape(width,...]
    unnamed x5 -> x0, local copies, waits for them, and re-layouts: 8.64 us -> none
    pallas_call x0 -> x1, Pallas kernels: none -> 2.28 us  [fused(): pl.pallas_call(functools.partial(place_kernel, len(results)), out_shape=[...]
where the time goes in v2:
time: 128 us; the launch traced here: 127 us
  Pallas kernels  127 us (99%)
    pallas_call x1, Pallas kernels, fused(): pl.pallas_call(fused_kernel, out_shape=[shape(span, width), shape(width,...  124 us

profile of v2, /device:TPU:0, one launch (start us, length us, event | category | flops | bytes accessed | tf_op | source)
XLA Modules:
  0.0 127.4 jit_solution(11877021815761440800)
XLA Ops:
  0.6 124.3 %shard_map.128 = (f32[384,256]{1,0:T(8,128)}, f32[256,256]{1,0:T(8,128)}, f32[256,256]{1,0:T(8,128)}, f32[256,256]{1,0:T(8,128)}, f32[8,64,256]{2,1,0:T(8,128)}) custom-call(f32[1536,3072]{1,0:T(8,128)} %matrix.1, f32[384,256]{1,0:T(8,128)} %panel_one.1, f32[384,256]{1,0:T(8,128)} %panel_two.1, s32[84,128]{1,0:T(8,128)} %bitcast.3, s32[72,128]{1,0:T(8,128)} %bitcast.4, ...), custom_call_target="tpu_custom_call" | custom-call | flops 14495514624 | bytes 18874368 | tf_op jit(solution)/shard_map/pallas_call | solution.py:784
  125.0 2.3 %shard_map.129 = (f32[384,256]{1,0:T(8,128)}, f32[256,256]{1,0:T(8,128)}, f32[256,256]{1,0:T(8,128)}, f32[256,256]{1,0:T(8,128)}, f32[8,64,256]{2,1,0:T(8,128)}) custom-call(f32[384,256]{1,0:T(8,128)} %get-tuple-element.10.refs_0_, f32[256,256]{1,0:T(8,128)} %get-tuple-element.11.refs_1_, f32[256,256]{1,0:T(8,128)} %get-tuple-element.12.refs_2_, ...), custom_call_target="tpu_custom_call" | custom-call | tf_op jit(solution)/shard_map/pallas_call | solution.py:863

commit v3 on v2

--- a/solution.py
+++ b/solution.py
@@ -292,7 +292,9 @@
     across = device(z, y, 1 - x, core)
     beside = device(z, 1 - y, x, core)
     near = device(upper * 2 + 1 - lower, y, x, core)
-    away = device((1 - upper) * 2 + lower, y, x, core)
+    inner = device(3 - z, y, x, core)
+    ends = upper == lower
+    middle = upper != lower
 
     def remote(source, target, sems, at, peer):
         return pltpu.make_async_remote_copy(
@@ -311,9 +313,8 @@
         copy.start()
 
     def fetch(step, which):
-        target_upper = lax.rem(upper + 1 + step // 2, 2)
-        target_lower = lax.rem(lower + 1 + step, 2)
-        target = (target_upper * 2 + target_lower) * 2 + lax.rem(1 - y + which, 2)
+        rank = jnp.where(ends, step, jnp.where(step == 0, 0, jnp.where(step == 3, 2, 5 - 2 * step)))
+        target = jnp.where(upper == 0, 3 - rank, rank) * 2 + lax.rem(1 - y + which, 2)
         return pltpu.make_async_copy(
             matrix.at[:, pl.ds(pl.multiple_of(target * span, LANES), span)], window.at[which], fetch_sem.at[which]
         )
@@ -492,44 +493,51 @@
         pl.when(step == 1)(lambda: climb_turned(1))
         return carry
 
-    def later_steps(at):
+    def later_steps(chunks, begin, end):
         def body(step, carry):
-            for which in range(2):
-                multiply(at, step, which)
+            for at in chunks:
+                for which in range(2):
+                    multiply(at, step, which)
             return carry
 
-        lax.fori_loop(0, 4, body, 0)
-
-    def major_copy(at, slot, peer):
-        return remote(mine.at[at, slot], major_in.at[at, slot], major_sem, (at, slot), peer)
-
-    def open_near(at):
-        pair_copy(at, 0).wait_recv()
-        mine[at, 0] = mine[at, 0] + pair_in[at, 0]
-        major_copy(at, 0, near).start()
-
-    def open_away(at):
-        pair_copy(at, 1).wait_recv()
-        mine[at, 1] = mine[at, 1] + pair_in[at, 1]
-        major_copy(at, 0, near).wait_recv()
-        mine[at, 1] = mine[at, 1] + major_in[at, 0]
-        major_copy(at, 1, away).start()
-
-    def close_near(at):
-        pair_copy(at, 2).wait_recv()
-        mine[at, 2] = mine[at, 2] + pair_in[at, 2]
-        major_copy(at, 2, near).start()
+        lax.fori_loop(begin, end, body, 0)
+
+    def major_copy(at, step):
+        slot = jnp.where(ends, (0, 2, 3)[step], (1, 3, 4)[step])
+        return pltpu.make_async_remote_copy(
+            src_ref=mine.at[at, step],
+            dst_ref=major_in.at[at, slot],
+            send_sem=major_sem.at[0, at, step],
+            recv_sem=major_sem.at[1, at, slot],
+            device_id=near if step == 1 else (jnp.where(ends, near[0], inner[0]), col),
+            device_id_type=MESH,
+        )
+
+    def arrived(at, slot):
+        pltpu.make_async_copy(mine.at[at, 0], major_in.at[at, slot], major_sem.at[1, at, slot]).wait()
+        return major_in[at, slot]
+
+    def forward(at, step):
+        pair_copy(at, step).wait_recv()
+        mine[at, step] = mine[at, step] + pair_in[at, step]
+
+        @pl.when(middle)
+        def _():
+            mine[at, step] = mine[at, step] + arrived(at, step)
+
+        major_copy(at, step).start()
 
     def collect(at):
         pair_copy(at, 3).wait_recv()
-        value = mine[at, 3] + pair_in[at, 3]
-        major_copy(at, 1, away).wait_recv()
-        major_copy(at, 2, near).wait_recv()
-        product[at] = value + (major_in[at, 1] + major_in[at, 2])
+        product[at] = (mine[at, 3] + pair_in[at, 3]) + arrived(at, 3)
+
+        @pl.when(middle)
+        def _():
+            product[at] = product[at] + arrived(at, 4)
 
     half = width // 2
-    share_of = (4 * half, 2 * half)
-    starts = (0, 4 * half)
+    share_of = (4 * half, half, half)
+    starts = (0, 4 * half, 5 * half)
     order = sorted(range(1, CHIPS), key=lambda offset: -min(offset, CHIPS - offset))
     plain, last = ((1,), (0,)), ((1,), (1,))
 
@@ -641,28 +649,38 @@
         for rank in range(CAP):
             tiles_here[rank, :, columns] = slot_value(col, rank)
 
-    first_total, second_total = Total(0), Total(1)
+    first_total, middle_total, second_total = Total(0), Total(1), Total(2)
 
     prepare(0)
     climb_turned(0)
     lax.fori_loop(0, 4, first_step, 0)
     prepare(1)
-    open_near(0)
-    later_steps(1)
-    close_near(0)
+    def only(where, *steps):
+        @pl.when(where)
+        def _():
+            for at, step in steps:
+                forward(at, step)
+
+    only(ends, (0, 0))
+    later_steps((1,), 0, 4)
+    only(middle, (0, 0))
+    only(ends, (0, 1))
+    prepare(2)
+    prepare(3)
+    only(ends, (0, 2))
+    later_steps((2, 3), 0, 2)
+    only(middle, (0, 1), (0, 2))
+    only(ends, (1, 0))
     pass_on(0)
-    prepare(2)
-    later_steps(2)
-    open_near(1)
-    open_away(0)
     pass_on(1)
-    close_near(1)
-    open_away(1)
+    only(ends, (1, 1))
     collect(0)
-    prepare(3)
-    open_near(2)
-    later_steps(3)
+    only(middle, (1, 0), (1, 1))
+    forward(1, 2)
+    only(ends, (2, 0))
     collect(1)
+    only(ends, (3, 0))
+    only(middle, (2, 0))
     one_row = mask_of(0, slots_of)
     two_row = mask_of(1, slots_of)
     inv_one_t[...] = -(jnp.concatenate([product[at] for at in range(per_panel)], axis=0) * one_row)
@@ -678,22 +696,29 @@
     outs = [pltpu.make_async_copy(inverse_one, inverse_one_out, out_sem.at[0])]
     outs[0].start()
     first_total.scatter()
-    open_away(2)
-    close_near(2)
-    open_near(3)
+    later_steps((2, 3), 2, 4)
+    only(middle, (3, 0))
+    forward(2, 1)
+    forward(3, 1)
+    first_total.gather()
+    forward(2, 2)
+    forward(3, 2)
     collect(2)
-    part_two_t[pl.ds(0, half), :] = -(product[2] * two_row)
-    send_tiles(0, (part_two_t[pl.ds(0, half), :] - correction[pl.ds(0, half), :]).T)
-    open_away(3)
-    close_near(3)
-    first_total.gather()
+    low_half, high_half = pl.ds(0, half), pl.ds(half, half)
+    part_two_t[low_half, :] = -(product[2] * two_row)
+    gram_left = exact(panel_two_t[...], part_two_t[low_half, :], last)
+    middle_total.begin([gram_left[:half], gram_left[half:]])
+    early = (part_two_t[low_half, :] - correction[low_half, :]).T
+    middle_total.scatter()
+    send_tiles(0, early)
     collect(3)
-    part_two_t[pl.ds(half, half), :] = -(product[3] * two_row)
-    gram_two = exact(panel_two_t[...], part_two_t[...], last)
-    second_total.begin(quarters(gram_two, upper_places))
+    part_two_t[high_half, :] = -(product[3] * two_row)
+    second_total.begin([exact(panel_two_t[high_half, :], part_two_t[high_half, :], last)])
+    late = (part_two_t[high_half, :] - correction[high_half, :]).T
+    second_total.scatter()
+    send_tiles(1, late)
+    middle_total.gather()
     first_total.finish()
-    second_total.scatter()
-    send_tiles(1, (part_two_t[pl.ds(half, half), :] - correction[pl.ds(half, half), :]).T)
 
     here = pltpu.make_async_copy(tiles_here, delivered.at[pl.ds(col * CAP, CAP)], out_sem.at[4])
     here.start()
@@ -720,10 +745,12 @@
     put(2, cross_two, cross_two_out)
     diag_two[...] = diag_two[...] + (exact(cross_total.T, above[...], plain) - exact(above_t, cross_value, plain))
     second_total.gather()
+    middle_total.finish()
+    middle_total.final.wait_recv()
+    tile = middle_total.tile
     second_total.finish()
     second_total.final.wait_recv()
-    tile = second_total.tile
-    diag_two[...] = diag_two[...] - square(tile(0), tile(1), tile(1).T, tile(2))
+    diag_two[...] = diag_two[...] - square(tile(0), tile(1).T, tile(1), second_total.tile(0))
     put(3, diag_two, diag_two_out)
 
     for copy in tile_copies:
@@ -744,15 +771,15 @@
 
     for copy in outs:
         copy.wait()
-    for copy in first_total.sent + second_total.sent + tile_copies:
+    for copy in first_total.sent + middle_total.sent + second_total.sent + tile_copies:
         copy.wait_send()
     for at in range(CHUNKS):
         for copy in (near_copy(at), far_copy(at), relay_copy(at)):
             copy.wait_send()
         for step in range(4):
             pair_copy(at, step).wait_send()
-        for slot, peer in enumerate((near, away, near)):
-            major_copy(at, slot, peer).wait_send()
+        for step in range(3):
+            major_copy(at, step).wait_send()
 
 
 def place_kernel(count, *refs):
@@ -812,7 +839,7 @@
             vmem(CHUNKS, 4, chunk, span),
             vmem(CHUNKS, 4, chunk, span),
             vmem(CHUNKS, 4, chunk, span),
-            vmem(CHUNKS, 3, chunk, span),
+            vmem(CHUNKS, 5, chunk, span),
             vmem(2, mask_rows, LANES),
             vmem(2, span, width),
             vmem(2, 2, span, width),
@@ -837,14 +864,14 @@
             dma((2, CHUNKS)),
             dma((2, CHUNKS)),
             dma((2, CHUNKS, 4)),
-            dma((2, CHUNKS, 3)),
-            dma((2, 2, 2)),
-            dma((2, 2, CHIPS - 1)),
-            dma((2, 2, CHIPS - 1)),
+            dma((2, CHUNKS, 5)),
+            dma((2, 3, 2)),
+            dma((2, 3, CHIPS - 1)),
+            dma((2, 3, CHIPS - 1)),
             dma((2, 2, COLS - 1)),
         ],
         compiler_params=pltpu.CompilerParams(
-            collective_id=3, has_side_effects=True, vmem_limit_bytes=54 * 2**20
+            collective_id=3, has_side_effects=True, vmem_limit_bytes=58 * 2**20
         ),
         cost_estimate=pl.CostEstimate(
             flops=12 * matrix.size * width, bytes_accessed=4 * matrix.size, transcendentals=0

time: 128 us -> 113 us (0.88)
  Pallas kernels: 127 us -> 111 us
    pallas_call x1, Pallas kernels: 124 us -> 109 us  [fused(): pl.pallas_call(fused_kernel, out_shape=[shape(span, width), shape(width,...]
where the time goes in v3:
time: 113 us; the launch traced here: 112 us
  Pallas kernels  111 us (98%)
    pallas_call x1, Pallas kernels, fused(): pl.pallas_call(fused_kernel, out_shape=[shape(span, width), shape(width,...  109 us
    pallas_call x1, Pallas kernels, fused(): pl.pallas_call(functools.partial(place_kernel, len(results)), out_shape=[...  2.28 us

profile of v3, /device:TPU:0, one launch (start us, length us, event | category | flops | bytes accessed | tf_op | source)
XLA Modules:
  0.0 111.6 jit_solution(706516661558363187)
XLA Ops:
  0.6 108.5 %shard_map.128 = (f32[384,256]{1,0:T(8,128)}, f32[256,256]{1,0:T(8,128)}, f32[256,256]{1,0:T(8,128)}, f32[256,256]{1,0:T(8,128)}, f32[8,64,256]{2,1,0:T(8,128)}) custom-call(f32[1536,3072]{1,0:T(8,128)} %matrix.1, f32[384,256]{1,0:T(8,128)} %panel_one.1, f32[384,256]{1,0:T(8,128)} %panel_two.1, s32[84,128]{1,0:T(8,128)} %bitcast.3, s32[72,128]{1,0:T(8,128)} %bitcast.4, ...), custom_call_target="tpu_custom_call" | custom-call | flops 14495514624 | bytes 18874368 | tf_op jit(solution)/shard_map/pallas_call | solution.py:811
  109.2 2.3 %shard_map.129 = (f32[384,256]{1,0:T(8,128)}, f32[256,256]{1,0:T(8,128)}, f32[256,256]{1,0:T(8,128)}, f32[256,256]{1,0:T(8,128)}, f32[8,64,256]{2,1,0:T(8,128)}) custom-call(f32[384,256]{1,0:T(8,128)} %get-tuple-element.10.refs_0_, f32[256,256]{1,0:T(8,128)} %get-tuple-element.11.refs_1_, f32[256,256]{1,0:T(8,128)} %get-tuple-element.12.refs_2_, ...), custom_call_target="tpu_custom_call" | custom-call | tf_op jit(solution)/shard_map/pallas_call | solution.py:890

commit v4 on v3

--- a/solution.py
+++ b/solution.py
@@ -270,9 +270,9 @@
     inverse_one_out, diag_one_out, cross_two_out, diag_two_out, delivered,
     inverse_one, diag_one, cross_two, diag_two, tiles_here,
     struct_one, struct_two, lower_one, above, lower_two, window, high, low, own, land, left, other, mine, pair_in, major_in, masks, turned, resident, product,
-    inv_one_t, part_two_t, panel_two_t, correction, packed, fold_in, fold, part_in, full, outgoing,
-    out_sem, small_sem, fetch_sem, own_sem, turn_sem, move_sem, near_gather, far_gather, relay_gather, pair_sem, major_sem, sum_sem, chip_sem,
-    spread_sem, tile_sem,
+    inv_one_t, part_two_t, panel_two_t, correction, packed, fold_in, fold, part_in, side, wide_sum, straight, full, outgoing,
+    out_sem, small_sem, fetch_sem, own_sem, turn_sem, move_sem, near_gather, far_gather, relay_gather, pair_sem, major_sem, sum_sem, line_sem,
+    direct_send, direct_recv, hand_send, hand_recv, tile_sem,
 ):
     row = lax.axis_index("row")
     col = lax.axis_index("col")
@@ -332,10 +332,14 @@
     for copy in small_copies:
         copy.start()
     barrier = pltpu.get_barrier_semaphore()
+
+    def greet_at(semaphore, peer):
+        pl.semaphore_signal(semaphore, inc=1, device_id=peer, device_id_type=MESH)
+
     devices = ROWS * COLS
     for offset in range(1, devices):
         flat = lax.rem(row * COLS + col + offset, devices)
-        pl.semaphore_signal(barrier, inc=1, device_id=(flat // COLS, lax.rem(flat, COLS)), device_id_type=MESH)
+        greet_at(barrier, (flat // COLS, lax.rem(flat, COLS)))
     for which in range(2):
         fetch(0, which).start()
     pl.semaphore_wait(barrier, devices - 1)
@@ -536,78 +540,167 @@
             product[at] = product[at] + arrived(at, 4)
 
     half = width // 2
-    share_of = (4 * half, half, half)
-    starts = (0, 4 * half, 5 * half)
-    order = sorted(range(1, CHIPS), key=lambda offset: -min(offset, CHIPS - offset))
     plain, last = ((1,), (0,)), ((1,), (1,))
-
-    def chip_at(offset):
-        flat = lax.rem(chip + offset, CHIPS)
-        return flat, device(flat // 4, lax.rem(flat // 2, 2), lax.rem(flat, 2), core)
-
-    class Total:
-        def __init__(self, at):
-            self.at, self.share, self.start = at, share_of[at], starts[at]
-            self.rows = self.share // CHIPS
-            self.base = 2 * self.start + core * self.share
+    def flipped(upper_at, lower_at, y_at, x_at):
+        z_at = jnp.where(upper_at, 1 - upper, upper) * 2 + jnp.where(lower_at, 1 - lower, lower)
+        return z_at, jnp.where(y_at, 1 - y, y), jnp.where(x_at, 1 - x, x)
+
+    def bits_of(offset):
+        return offset // 8, offset // 4 % 2, offset // 2 % 2, offset % 2
+
+    far_chips = sorted(range(1, CHIPS), key=lambda offset: -sum(w * b for w, b in zip((2.2, 1, 1, 1), bits_of(offset))))
+
+    side_here = lax.rem(x + y, 2)
+    opposite = device(z, 1 - y, 1 - x, core)
+
+    class LineTotal:
+        share = 7 * half // 2
+        wide = share // 2
+        rows = wide // 4
+
+        def __init__(self):
+            self.base = core * self.share
             self.half_rows = pl.ds(self.base, self.share)
+            self.wide_rows = pl.ds(self.base + side_here * self.wide, self.wide)
+            self.mine_rows = pl.ds(self.base + side_here * self.wide + z * self.rows, self.rows)
             self.sent = []
 
-        def partner_copy(self, stage, source, target):
-            copy = remote(source, target, sum_sem, (self.at, stage), partner)
+        def launch(self, *copy):
+            copy = remote(*copy)
+            copy.start()
             self.sent.append(copy)
-            copy.start()
             return copy
 
         def begin(self, tiles):
-            for at in range(2 * self.share // half):
-                tile = tiles[at] if at < len(tiles) else jnp.zeros((half, half), jnp.float32)
-                packed[pl.ds(2 * self.start + at * half, half), :] = tile
-            theirs = pl.ds(2 * self.start + (1 - core) * self.share, self.share)
-            self.first = self.partner_copy(0, packed.at[theirs], fold_in.at[pl.ds(self.start, self.share)])
+            for at, tile in enumerate(tiles):
+                packed[pl.ds(at * half, half), :] = tile
+            theirs = pl.ds((1 - core) * self.share, self.share)
+            self.first = self.launch(packed.at[theirs], fold_in, sum_sem, (0,), partner)
 
         def scatter(self):
             self.first.wait_recv()
-            rows = pl.ds(self.start, self.share)
-            fold[rows, :] = packed[self.half_rows, :] + fold_in[rows, :]
-            self.copies = []
-            for offset in order:
-                flat, peer = chip_at(offset)
-                copy = remote(
-                    fold.at[pl.ds(self.start + flat * self.rows, self.rows)],
-                    part_in.at[offset - 1, pl.ds(self.start // CHIPS, self.rows)],
-                    chip_sem,
-                    (self.at, offset - 1),
-                    peer,
-                )
-                copy.start()
-                self.copies.append(copy)
-
-        def gather(self):
+            fold[...] = packed[self.half_rows, :] + fold_in[...]
+            theirs = pl.ds((1 - side_here) * self.wide, self.wide)
+            self.second = self.launch(fold.at[theirs], wide_sum.at[1], sum_sem, (3,), across)
+
+        def line(self):
+            for at, (upper_at, lower_at) in enumerate(((1, 1), (1, 0), (0, 1))):
+                z_at = flipped(upper_at, lower_at, 0, 0)[0]
+                yield at, z_at, device(z_at, y, x, core)
+
+        def climb(self):
+            self.second.wait_recv()
+            wide_sum[0] = fold[pl.ds(side_here * self.wide, self.wide), :] + wide_sum[1]
+            self.copies = [
+                self.launch(wide_sum.at[0, pl.ds(z_at * self.rows, self.rows)], part_in.at[at], line_sem, (0, at), peer)
+                for at, z_at, peer in self.line()
+            ]
+
+        def cross(self):
             for copy in self.copies:
                 copy.wait_recv()
-            value = fold[pl.ds(self.start + chip * self.rows, self.rows), :]
-            for slot in range(CHIPS - 1):
-                value = value + part_in[slot, pl.ds(self.start // CHIPS, self.rows), :]
-            mine_rows = pl.ds(self.base + chip * self.rows, self.rows)
-            full[mine_rows, :] = value
-            self.sent += self.copies
-            self.copies = []
-            for offset in order:
-                copy = remote(
-                    full.at[mine_rows], full.at[mine_rows], spread_sem, (self.at, offset - 1), chip_at(offset)[1]
-                )
-                copy.start()
-                self.copies.append(copy)
-
-        def finish(self):
+            side[0] = (wide_sum[0, pl.ds(z * self.rows, self.rows), :] + part_in[0]) + (part_in[1] + part_in[2])
+            self.crossing = self.launch(side.at[0], side.at[1], sum_sem, (2,), opposite)
+
+        def spread(self):
+            self.crossing.wait_recv()
+            full[self.mine_rows, :] = side[0] + side[1]
+            target = full.at[self.mine_rows]
+            self.copies = [self.launch(target, target, line_sem, (1, at), peer) for at, _, peer in self.line()]
+
+        def widen(self):
             for copy in self.copies:
                 copy.wait_recv()
-            self.final = self.partner_copy(1, full.at[self.half_rows], full.at[self.half_rows])
-            self.sent += self.copies
+            target = full.at[self.wide_rows]
+            self.second = self.launch(target, target, sum_sem, (4,), across)
+
+        def finish(self):
+            self.second.wait_recv()
+            target = full.at[self.half_rows]
+            self.final = self.launch(target, target, sum_sem, (1,), partner)
 
         def tile(self, at):
-            return full[pl.ds(2 * self.start + at * half, half), :]
+            return full[pl.ds(at * half, half), :]
+
+    owner_here = core == x
+
+    class DirectTotal:
+        def __init__(self, at, start, blocks):
+            self.at, self.start, self.rows = at, start, blocks * half // CHIPS
+            self.mine_rows = pl.ds(start + chip * self.rows, self.rows)
+
+        def place(self, offset, core_at=None):
+            z_at, y_at, x_at = flipped(*bits_of(offset))
+            return (z_at * 2 + y_at) * 2 + x_at, device(z_at, y_at, x_at, x_at if core_at is None else core_at)
+
+        def sending(self, offset):
+            flat, peer = self.place(offset)
+            return pltpu.make_async_remote_copy(
+                src_ref=packed.at[pl.ds(self.start + flat * self.rows, self.rows)],
+                dst_ref=straight.at[self.at, offset * 2 + core, pl.ds(0, self.rows)],
+                send_sem=direct_send.at[self.at, offset],
+                recv_sem=direct_recv.at[self.at, offset * 2 + core],
+                device_id=peer,
+                device_id_type=MESH,
+            )
+
+        def handing(self, offset, core_at):
+            peer = partner if core_at is None else self.place(offset, core_at)[1]
+            return pltpu.make_async_remote_copy(
+                src_ref=full.at[self.mine_rows],
+                dst_ref=full.at[self.mine_rows],
+                send_sem=hand_send.at[self.at, offset * 2 + (core_at or 0)],
+                recv_sem=hand_recv.at[self.at, offset],
+                device_id=peer,
+                device_id_type=MESH,
+            )
+
+        def hands(self):
+            return [self.handing(offset, core_at) for offset in far_chips for core_at in range(2)] + [
+                self.handing(0, None)
+            ]
+
+        def begin(self, tiles):
+            for at, tile in enumerate(tiles):
+                packed[pl.ds(self.start + at * half, half), :] = tile
+            for offset in far_chips:
+                self.sending(offset).start()
+            pl.when(jnp.logical_not(owner_here))(lambda: self.sending(0).start())
+
+        def spread(self):
+            @pl.when(owner_here)
+            def _():
+                rows = pl.ds(0, self.rows)
+
+                def landed(slot):
+                    target = straight.at[self.at, slot, rows]
+                    pltpu.make_async_copy(target, target, direct_recv.at[self.at, slot]).wait()
+                    return straight[self.at, slot, rows, :]
+
+                value = packed[self.mine_rows, :] + landed(1 - core)
+                for slot in range(2, 2 * CHIPS):
+                    value = value + landed(slot)
+                full[self.mine_rows, :] = value
+                for copy in self.hands():
+                    copy.start()
+
+        def finish(self):
+            for offset in range(1, CHIPS):
+                self.handing(offset, 0).wait_recv()
+            pl.when(jnp.logical_not(owner_here))(lambda: self.handing(0, None).wait_recv())
+
+        def drain(self):
+            for offset in range(1, CHIPS):
+                self.sending(offset).wait_send()
+            pl.when(jnp.logical_not(owner_here))(lambda: self.sending(0).wait_send())
+
+            @pl.when(owner_here)
+            def _():
+                for copy in self.hands():
+                    copy.wait_send()
+
+        def tile(self, at):
+            return full[pl.ds(self.start + at * half, half), :]
 
     def quarters(value, places):
         return [value[i * half : (i + 1) * half, j * half : (j + 1) * half] for i, j in places]
@@ -649,7 +742,8 @@
         for rank in range(CAP):
             tiles_here[rank, :, columns] = slot_value(col, rank)
 
-    first_total, middle_total, second_total = Total(0), Total(1), Total(2)
+    first_total = LineTotal()
+    middle_total, second_total = DirectTotal(0, 7 * half, 2), DirectTotal(1, 9 * half, 1)
 
     prepare(0)
     climb_turned(0)
@@ -696,28 +790,30 @@
     outs = [pltpu.make_async_copy(inverse_one, inverse_one_out, out_sem.at[0])]
     outs[0].start()
     first_total.scatter()
-    later_steps((2, 3), 2, 4)
-    only(middle, (3, 0))
-    forward(2, 1)
+    later_steps((2, 3), 2, 3)
+    only(ends, (2, 1))
+    only(middle, (3, 0), (2, 1))
+    later_steps((2, 3), 3, 4)
+    first_total.climb()
     forward(3, 1)
-    first_total.gather()
     forward(2, 2)
+    first_total.cross()
     forward(3, 2)
     collect(2)
+    first_total.spread()
     low_half, high_half = pl.ds(0, half), pl.ds(half, half)
     part_two_t[low_half, :] = -(product[2] * two_row)
     gram_left = exact(panel_two_t[...], part_two_t[low_half, :], last)
     middle_total.begin([gram_left[:half], gram_left[half:]])
-    early = (part_two_t[low_half, :] - correction[low_half, :]).T
-    middle_total.scatter()
-    send_tiles(0, early)
+    send_tiles(0, (part_two_t[low_half, :] - correction[low_half, :]).T)
     collect(3)
     part_two_t[high_half, :] = -(product[3] * two_row)
     second_total.begin([exact(panel_two_t[high_half, :], part_two_t[high_half, :], last)])
     late = (part_two_t[high_half, :] - correction[high_half, :]).T
-    second_total.scatter()
+    middle_total.spread()
+    first_total.widen()
     send_tiles(1, late)
-    middle_total.gather()
+    second_total.spread()
     first_total.finish()
 
     here = pltpu.make_async_copy(tiles_here, delivered.at[pl.ds(col * CAP, CAP)], out_sem.at[4])
@@ -744,12 +840,9 @@
     cross_two[...] = cross_value
     put(2, cross_two, cross_two_out)
     diag_two[...] = diag_two[...] + (exact(cross_total.T, above[...], plain) - exact(above_t, cross_value, plain))
-    second_total.gather()
     middle_total.finish()
-    middle_total.final.wait_recv()
     tile = middle_total.tile
     second_total.finish()
-    second_total.final.wait_recv()
     diag_two[...] = diag_two[...] - square(tile(0), tile(1).T, tile(1), second_total.tile(0))
     put(3, diag_two, diag_two_out)
 
@@ -771,7 +864,9 @@
 
     for copy in outs:
         copy.wait()
-    for copy in first_total.sent + middle_total.sent + second_total.sent + tile_copies:
+    middle_total.drain()
+    second_total.drain()
+    for copy in first_total.sent + tile_copies:
         copy.wait_send()
     for at in range(CHUNKS):
         for copy in (near_copy(at), far_copy(at), relay_copy(at)):
@@ -800,7 +895,7 @@
     span, width = panel_one.shape
     chunk = 2 * width // CHUNKS
     tile_count = tile_owner.shape[0]
-    share = 6 * (width // 2)
+    share = 7 * (width // 2) // 2
     mask_rows = -(-(COLS + 1) * (span // LANES) // 8) * 8
     dma = pltpu.SemaphoreType.DMA
     vmem = lambda *shape: pltpu.VMEM(shape, jnp.float32)
@@ -848,11 +943,14 @@
             vmem(width, span),
             vmem(width, span),
             vmem(width, span),
-            vmem(2 * share, LANES),
+            vmem(10 * (width // 2), LANES),
             vmem(share, LANES),
             vmem(share, LANES),
-            vmem(CHIPS - 1, share // CHIPS, LANES),
-            vmem(2 * share, LANES),
+            vmem(3, share // 8, LANES),
+            vmem(2, share // 8, LANES),
+            vmem(2, share // 2, LANES),
+            vmem(2, 2 * CHIPS, width // CHIPS, LANES),
+            vmem(10 * (width // 2), LANES),
             vmem(COLS - 1, CAP, span // tile_count, width),
             dma((5,)),
             dma((5,)),
@@ -865,9 +963,12 @@
             dma((2, CHUNKS)),
             dma((2, CHUNKS, 4)),
             dma((2, CHUNKS, 5)),
-            dma((2, 3, 2)),
-            dma((2, 3, CHIPS - 1)),
-            dma((2, 3, CHIPS - 1)),
+            dma((2, 5)),
+            dma((2, 2, 3)),
+            dma((2, CHIPS)),
+            dma((2, 2 * CHIPS)),
+            dma((2, 2 * CHIPS)),
+            dma((2, CHIPS)),
             dma((2, 2, COLS - 1)),
         ],
         compiler_params=pltpu.CompilerParams(

time: 113 us -> 107 us (0.947)
  Pallas kernels: 111 us -> 106 us
    pallas_call x1, Pallas kernels: 109 us -> 104 us  [fused(): pl.pallas_call(fused_kernel, out_shape=[shape(span, width), shape(width,...]
where the time goes in v4:
time: 107 us
  Pallas kernels  106 us (99%)
    pallas_call x1, Pallas kernels, fused(): pl.pallas_call(fused_kernel, out_shape=[shape(span, width), shape(width,...  104 us
    pallas_call x1, Pallas kernels, fused(): pl.pallas_call(functools.partial(place_kernel, len(results)), out_shape=[...  2.28 us

profile of v4, /device:TPU:0, one launch (start us, length us, event | category | flops | bytes accessed | tf_op | source)
XLA Modules:
  0.0 106.6 jit_solution(3172822765813007921)
XLA Ops:
  0.6 103.6 %shard_map.128 = (f32[384,256]{1,0:T(8,128)}, f32[256,256]{1,0:T(8,128)}, f32[256,256]{1,0:T(8,128)}, f32[256,256]{1,0:T(8,128)}, f32[8,64,256]{2,1,0:T(8,128)}) custom-call(f32[1536,3072]{1,0:T(8,128)} %matrix.1, f32[384,256]{1,0:T(8,128)} %panel_one.1, f32[384,256]{1,0:T(8,128)} %panel_two.1, s32[84,128]{1,0:T(8,128)} %bitcast.3, s32[72,128]{1,0:T(8,128)} %bitcast.4, ...), custom_call_target="tpu_custom_call" | custom-call | flops 14495514624 | bytes 18874368 | tf_op jit(solution)/shard_map/pallas_call | solution.py:906
  104.2 2.3 %shard_map.129 = (f32[384,256]{1,0:T(8,128)}, f32[256,256]{1,0:T(8,128)}, f32[256,256]{1,0:T(8,128)}, f32[256,256]{1,0:T(8,128)}, f32[8,64,256]{2,1,0:T(8,128)}) custom-call(f32[384,256]{1,0:T(8,128)} %get-tuple-element.10.refs_0_, f32[256,256]{1,0:T(8,128)} %get-tuple-element.11.refs_1_, f32[256,256]{1,0:T(8,128)} %get-tuple-element.12.refs_2_, ...), custom_call_target="tpu_custom_call" | custom-call | tf_op jit(solution)/shard_map/pallas_call | solution.py:991

commit v5 on v4

--- a/solution.py
+++ b/solution.py
@@ -271,7 +271,7 @@
     inverse_one, diag_one, cross_two, diag_two, tiles_here,
     struct_one, struct_two, lower_one, above, lower_two, window, high, low, own, land, left, other, mine, pair_in, major_in, masks, turned, resident, product,
     inv_one_t, part_two_t, panel_two_t, correction, packed, fold_in, fold, part_in, side, wide_sum, straight, full, outgoing,
-    out_sem, small_sem, fetch_sem, own_sem, turn_sem, move_sem, near_gather, far_gather, relay_gather, pair_sem, major_sem, sum_sem, line_sem,
+    out_sem, small_sem, fetch_sem, own_sem, turn_sem, move_sem, flow_sem, gather_sem, pair_sem, major_sem, sum_sem, line_sem,
     direct_send, direct_recv, hand_send, hand_recv, tile_sem,
 ):
     row = lax.axis_index("row")
@@ -349,15 +349,30 @@
     def piece(at):
         return own.at[at // per_panel, :, pl.ds(at % per_panel * chunk, chunk)]
 
+    def flow(kind, source, target, recv_sem, peer):
+        return pltpu.make_async_remote_copy(
+            src_ref=source,
+            dst_ref=target,
+            send_sem=flow_sem.at[kind],
+            recv_sem=recv_sem,
+            device_id=peer,
+            device_id_type=MESH,
+        )
+
+    def take(like, semaphore):
+        pltpu.make_async_copy(like, like, semaphore).wait()
+
     def far_copy(at, source=None):
-        return remote(land.at[0, at] if source is None else source, land.at[col, at], far_gather, (at,), across)
+        source = land.at[0, at] if source is None else source
+        return flow(0, source, land.at[col, at], gather_sem.at[0, at], across)
 
     def near_copy(at, source=None):
-        return remote(land.at[0, at] if source is None else source, land.at[col, at], near_gather, (at,), partner)
+        source = land.at[0, at] if source is None else source
+        return flow(1, source, land.at[col, at], gather_sem.at[1, at], partner)
 
     def relay_copy(at):
         slot = (1 - x) * 2 + core
-        return remote(land.at[slot, at], land.at[slot, at], relay_gather, (at,), partner)
+        return flow(2, land.at[slot, at], land.at[slot, at], gather_sem.at[2, at], partner)
 
     turns = core != y
     direct = jnp.where(x == upper, 0, 1)
@@ -465,7 +480,7 @@
             left[at, pl.ds(chunk, chunk), columns] = (value - upper_part.astype(jnp.float32)).astype(jnp.bfloat16)
 
     def pair_copy(at, step):
-        return remote(other.at[at, step], pair_in.at[at, step], pair_sem, (at, step), beside)
+        return flow(3, other.at[at, step], pair_in.at[at, step], pair_sem.at[at, step], beside)
 
     def multiply(at, step, which):
         target = step * 2 + which
@@ -508,17 +523,11 @@
 
     def major_copy(at, step):
         slot = jnp.where(ends, (0, 2, 3)[step], (1, 3, 4)[step])
-        return pltpu.make_async_remote_copy(
-            src_ref=mine.at[at, step],
-            dst_ref=major_in.at[at, slot],
-            send_sem=major_sem.at[0, at, step],
-            recv_sem=major_sem.at[1, at, slot],
-            device_id=near if step == 1 else (jnp.where(ends, near[0], inner[0]), col),
-            device_id_type=MESH,
-        )
+        peer = near if step == 1 else (jnp.where(ends, near[0], inner[0]), col)
+        return flow(4, mine.at[at, step], major_in.at[at, slot], major_sem.at[at, slot], peer)
 
     def arrived(at, slot):
-        pltpu.make_async_copy(mine.at[at, 0], major_in.at[at, slot], major_sem.at[1, at, slot]).wait()
+        pltpu.make_async_copy(mine.at[at, 0], major_in.at[at, slot], major_sem.at[at, slot]).wait()
         return major_in[at, slot]
 
     def forward(at, step):
@@ -638,8 +647,8 @@
             return pltpu.make_async_remote_copy(
                 src_ref=packed.at[pl.ds(self.start + flat * self.rows, self.rows)],
                 dst_ref=straight.at[self.at, offset * 2 + core, pl.ds(0, self.rows)],
-                send_sem=direct_send.at[self.at, offset],
-                recv_sem=direct_recv.at[self.at, offset * 2 + core],
+                send_sem=direct_send.at[self.at, 0 if offset else 1],
+                recv_sem=direct_recv.at[self.at],
                 device_id=peer,
                 device_id_type=MESH,
             )
@@ -649,8 +658,8 @@
             return pltpu.make_async_remote_copy(
                 src_ref=full.at[self.mine_rows],
                 dst_ref=full.at[self.mine_rows],
-                send_sem=hand_send.at[self.at, offset * 2 + (core_at or 0)],
-                recv_sem=hand_recv.at[self.at, offset],
+                send_sem=hand_send.at[self.at],
+                recv_sem=hand_recv.at[self.at, 0 if offset else 1],
                 device_id=peer,
                 device_id_type=MESH,
             )
@@ -671,33 +680,25 @@
             @pl.when(owner_here)
             def _():
                 rows = pl.ds(0, self.rows)
-
-                def landed(slot):
-                    target = straight.at[self.at, slot, rows]
-                    pltpu.make_async_copy(target, target, direct_recv.at[self.at, slot]).wait()
-                    return straight[self.at, slot, rows, :]
-
-                value = packed[self.mine_rows, :] + landed(1 - core)
+                take(straight.at[self.at, pl.ds(0, 2 * CHIPS - 1), rows], direct_recv.at[self.at])
+                value = packed[self.mine_rows, :] + straight[self.at, 1 - core, rows, :]
                 for slot in range(2, 2 * CHIPS):
-                    value = value + landed(slot)
+                    value = value + straight[self.at, slot, rows, :]
                 full[self.mine_rows, :] = value
                 for copy in self.hands():
                     copy.start()
 
+        def many(self, count):
+            return packed.at[pl.ds(0, count * self.rows)]
+
         def finish(self):
-            for offset in range(1, CHIPS):
-                self.handing(offset, 0).wait_recv()
+            take(self.many(CHIPS - 1), hand_recv.at[self.at, 0])
             pl.when(jnp.logical_not(owner_here))(lambda: self.handing(0, None).wait_recv())
 
         def drain(self):
-            for offset in range(1, CHIPS):
-                self.sending(offset).wait_send()
+            take(self.many(CHIPS - 1), direct_send.at[self.at, 0])
             pl.when(jnp.logical_not(owner_here))(lambda: self.sending(0).wait_send())
-
-            @pl.when(owner_here)
-            def _():
-                for copy in self.hands():
-                    copy.wait_send()
+            pl.when(owner_here)(lambda: take(self.many(2 * CHIPS - 1), hand_send.at[self.at]))
 
         def tile(self, at):
             return full[pl.ds(self.start + at * half, half), :]
@@ -810,8 +811,8 @@
     part_two_t[high_half, :] = -(product[3] * two_row)
     second_total.begin([exact(panel_two_t[high_half, :], part_two_t[high_half, :], last)])
     late = (part_two_t[high_half, :] - correction[high_half, :]).T
+    first_total.widen()
     middle_total.spread()
-    first_total.widen()
     send_tiles(1, late)
     second_total.spread()
     first_total.finish()
@@ -829,6 +830,28 @@
         return jnp.concatenate(
             [jnp.concatenate([first, second], axis=1), jnp.concatenate([third, fourth], axis=1)], axis=0
         )
+
+    for copy in tile_copies:
+        copy.wait()
+
+    for panel in range(2):
+
+        @pl.when(turns)
+        def _():
+            turn[panel].wait_send()
+
+        @pl.when(jnp.logical_not(turns))
+        def _():
+            end_climb(own, panel, 0, y)
+            end_climb(turned, panel, 1, 1 - y)
+
+        pl.when(relays_move)(lambda: passed[panel].wait_send())
+
+    middle_total.drain()
+    for copy in first_total.sent[:-1]:
+        copy.wait_send()
+    for kind, like in enumerate((own, own, land.at[0], other, mine.at[:, pl.ds(0, 3)])):
+        take(like, flow_sem.at[kind])
 
     first_total.final.wait_recv()
     tile = first_total.tile
@@ -846,35 +869,10 @@
     diag_two[...] = diag_two[...] - square(tile(0), tile(1).T, tile(1), second_total.tile(0))
     put(3, diag_two, diag_two_out)
 
-    for copy in tile_copies:
-        copy.wait_recv()
-
-    for panel in range(2):
-
-        @pl.when(turns)
-        def _():
-            turn[panel].wait_send()
-
-        @pl.when(jnp.logical_not(turns))
-        def _():
-            end_climb(own, panel, 0, y)
-            end_climb(turned, panel, 1, 1 - y)
-
-        pl.when(relays_move)(lambda: passed[panel].wait_send())
-
     for copy in outs:
         copy.wait()
-    middle_total.drain()
     second_total.drain()
-    for copy in first_total.sent + tile_copies:
-        copy.wait_send()
-    for at in range(CHUNKS):
-        for copy in (near_copy(at), far_copy(at), relay_copy(at)):
-            copy.wait_send()
-        for step in range(4):
-            pair_copy(at, step).wait_send()
-        for step in range(3):
-            major_copy(at, step).wait_send()
+    first_total.final.wait_send()
 
 
 def place_kernel(count, *refs):
@@ -958,17 +956,16 @@
             dma((2,)),
             dma((2, 2)),
             dma((2, 2, 3)),
-            dma((2, CHUNKS)),
-            dma((2, CHUNKS)),
-            dma((2, CHUNKS)),
-            dma((2, CHUNKS, 4)),
-            dma((2, CHUNKS, 5)),
+            dma((5,)),
+            dma((3, CHUNKS)),
+            dma((CHUNKS, 4)),
+            dma((CHUNKS, 5)),
             dma((2, 5)),
             dma((2, 2, 3)),
-            dma((2, CHIPS)),
-            dma((2, 2 * CHIPS)),
-            dma((2, 2 * CHIPS)),
-            dma((2, CHIPS)),
+            dma((2, 2)),
+            dma((2,)),
+            dma((2,)),
+            dma((2, 2)),
             dma((2, 2, COLS - 1)),
         ],
         compiler_params=pltpu.CompilerParams(

time: 107 us -> 104 us (0.972)
  Pallas kernels: 106 us -> 103 us
    pallas_call x1, Pallas kernels: 104 us -> 101 us  [fused(): pl.pallas_call(fused_kernel, out_shape=[shape(span, width), shape(width,...]
where the time goes in v5:
time: 104 us
  Pallas kernels  103 us (99%)
    pallas_call x1, Pallas kernels, fused(): pl.pallas_call(fused_kernel, out_shape=[shape(span, width), shape(width,...  101 us
    pallas_call x1, Pallas kernels, fused(): pl.pallas_call(functools.partial(place_kernel, len(results)), out_shape=[...  2.28 us

profile of v5, /device:TPU:0, one launch (start us, length us, event | category | flops | bytes accessed | tf_op | source)
XLA Modules:
  0.0 104.0 jit_solution(12136804024072669207)
XLA Ops:
  0.6 100.9 %shard_map.128 = (f32[384,256]{1,0:T(8,128)}, f32[256,256]{1,0:T(8,128)}, f32[256,256]{1,0:T(8,128)}, f32[256,256]{1,0:T(8,128)}, f32[8,64,256]{2,1,0:T(8,128)}) custom-call(f32[1536,3072]{1,0:T(8,128)} %matrix.1, f32[384,256]{1,0:T(8,128)} %panel_one.1, f32[384,256]{1,0:T(8,128)} %panel_two.1, s32[84,128]{1,0:T(8,128)} %bitcast.3, s32[72,128]{1,0:T(8,128)} %bitcast.4, ...), custom_call_target="tpu_custom_call" | custom-call | flops 14495514624 | bytes 18874368 | tf_op jit(solution)/shard_map/pallas_call | solution.py:904
  101.6 2.3 %shard_map.129 = (f32[384,256]{1,0:T(8,128)}, f32[256,256]{1,0:T(8,128)}, f32[256,256]{1,0:T(8,128)}, f32[256,256]{1,0:T(8,128)}, f32[8,64,256]{2,1,0:T(8,128)}) custom-call(f32[384,256]{1,0:T(8,128)} %get-tuple-element.10.refs_0_, f32[256,256]{1,0:T(8,128)} %get-tuple-element.11.refs_1_, f32[256,256]{1,0:T(8,128)} %get-tuple-element.12.refs_2_, ...), custom_call_target="tpu_custom_call" | custom-call | tf_op jit(solution)/shard_map/pallas_call | solution.py:988

commit v6 on v5

--- a/solution.py
+++ b/solution.py
@@ -796,12 +796,12 @@
     only(middle, (3, 0), (2, 1))
     later_steps((2, 3), 3, 4)
     first_total.climb()
-    forward(3, 1)
-    forward(2, 2)
+    only(ends, (3, 1), (2, 2))
+    only(middle, (2, 2), (3, 1))
     first_total.cross()
     forward(3, 2)
+    first_total.spread()
     collect(2)
-    first_total.spread()
     low_half, high_half = pl.ds(0, half), pl.ds(half, half)
     part_two_t[low_half, :] = -(product[2] * two_row)
     gram_left = exact(panel_two_t[...], part_two_t[low_half, :], last)
@@ -812,8 +812,8 @@
     second_total.begin([exact(panel_two_t[high_half, :], part_two_t[high_half, :], last)])
     late = (part_two_t[high_half, :] - correction[high_half, :]).T
     first_total.widen()
+    send_tiles(1, late)
     middle_total.spread()
-    send_tiles(1, late)
     second_total.spread()
     first_total.finish()
 
@@ -831,9 +831,6 @@
             [jnp.concatenate([first, second], axis=1), jnp.concatenate([third, fourth], axis=1)], axis=0
         )
 
-    for copy in tile_copies:
-        copy.wait()
-
     for panel in range(2):
 
         @pl.when(turns)
@@ -847,7 +844,6 @@
 
         pl.when(relays_move)(lambda: passed[panel].wait_send())
 
-    middle_total.drain()
     for copy in first_total.sent[:-1]:
         copy.wait_send()
     for kind, like in enumerate((own, own, land.at[0], other, mine.at[:, pl.ds(0, 3)])):
@@ -869,8 +865,11 @@
     diag_two[...] = diag_two[...] - square(tile(0), tile(1).T, tile(1), second_total.tile(0))
     put(3, diag_two, diag_two_out)
 
+    for copy in tile_copies:
+        copy.wait()
     for copy in outs:
         copy.wait()
+    middle_total.drain()
     second_total.drain()
     first_total.final.wait_send()
 

time: 104 us -> 104 us (level)
  no operation moved by 1% of the time
where the time goes in v6:
time: 104 us
  Pallas kernels  103 us (99%)
    pallas_call x1, Pallas kernels, fused(): pl.pallas_call(fused_kernel, out_shape=[shape(span, width), shape(width,...  101 us
    pallas_call x1, Pallas kernels, fused(): pl.pallas_call(functools.partial(place_kernel, len(results)), out_shape=[...  2.28 us

profile of v6, /device:TPU:0, one launch (start us, length us, event | category | flops | bytes accessed | tf_op | source)
XLA Modules:
  0.0 104.0 jit_solution(12369026241282901492)
XLA Ops:
  0.6 100.9 %shard_map.128 = (f32[384,256]{1,0:T(8,128)}, f32[256,256]{1,0:T(8,128)}, f32[256,256]{1,0:T(8,128)}, f32[256,256]{1,0:T(8,128)}, f32[8,64,256]{2,1,0:T(8,128)}) custom-call(f32[1536,3072]{1,0:T(8,128)} %matrix.1, f32[384,256]{1,0:T(8,128)} %panel_one.1, f32[384,256]{1,0:T(8,128)} %panel_two.1, s32[84,128]{1,0:T(8,128)} %bitcast.3, s32[72,128]{1,0:T(8,128)} %bitcast.4, ...), custom_call_target="tpu_custom_call" | custom-call | flops 14495514624 | bytes 18874368 | tf_op jit(solution)/shard_map/pallas_call | solution.py:903
  101.6 2.3 %shard_map.129 = (f32[384,256]{1,0:T(8,128)}, f32[256,256]{1,0:T(8,128)}, f32[256,256]{1,0:T(8,128)}, f32[256,256]{1,0:T(8,128)}, f32[8,64,256]{2,1,0:T(8,128)}) custom-call(f32[384,256]{1,0:T(8,128)} %get-tuple-element.10.refs_0_, f32[256,256]{1,0:T(8,128)} %get-tuple-element.11.refs_1_, f32[256,256]{1,0:T(8,128)} %get-tuple-element.12.refs_2_, ...), custom_call_target="tpu_custom_call" | custom-call | tf_op jit(solution)/shard_map/pallas_call | solution.py:987

commit v7 on v6

--- a/solution.py
+++ b/solution.py
@@ -337,9 +337,11 @@
         pl.semaphore_signal(semaphore, inc=1, device_id=peer, device_id_type=MESH)
 
     devices = ROWS * COLS
-    for offset in range(1, devices):
-        flat = lax.rem(row * COLS + col + offset, devices)
-        greet_at(barrier, (flat // COLS, lax.rem(flat, COLS)))
+    for offset in range(devices - 1, 0, -1):
+        up, below, over_y, over_x, over_core = (offset // size % 2 for size in (16, 8, 4, 2, 1))
+        z_at = (1 - upper if up else upper) * 2 + (1 - lower if below else lower)
+        there = (1 - y if over_y else y, 1 - x if over_x else x, 1 - core if over_core else core)
+        greet_at(barrier, device(z_at, *there))
     for which in range(2):
         fetch(0, which).start()
     pl.semaphore_wait(barrier, devices - 1)
@@ -878,9 +880,9 @@
     sources, targets, buffers, sems = refs[:count], refs[count : 2 * count], refs[2 * count : -1], refs[-1]
     loads = [pltpu.make_async_copy(sources[at], buffers[at], sems.at[0, at]) for at in range(count)]
     stores = [pltpu.make_async_copy(buffers[at], targets[at], sems.at[1, at]) for at in range(count)]
-    for copy in loads:
+    for copy in reversed(loads):
         copy.start()
-    for load, store in zip(loads, stores):
+    for load, store in reversed(list(zip(loads, stores))):
         load.wait()
         store.start()
     for copy in stores:

time: 104 us -> 104 us (level)
  no operation moved by 1% of the time
where the time goes in v7:
time: 104 us
  Pallas kernels  103 us (99%)
    pallas_call x1, Pallas kernels, fused(): pl.pallas_call(fused_kernel, out_shape=[shape(span, width), shape(width,...  101 us
    pallas_call x1, Pallas kernels, fused(): pl.pallas_call(functools.partial(place_kernel, len(results)), out_shape=[...  2.31 us

profile of v7, /device:TPU:0, one launch (start us, length us, event | category | flops | bytes accessed | tf_op | source)
XLA Modules:
  0.0 104.0 jit_solution(3764883570029363936)
XLA Ops:
  0.6 100.9 %shard_map.128 = (f32[384,256]{1,0:T(8,128)}, f32[256,256]{1,0:T(8,128)}, f32[256,256]{1,0:T(8,128)}, f32[256,256]{1,0:T(8,128)}, f32[8,64,256]{2,1,0:T(8,128)}) custom-call(f32[1536,3072]{1,0:T(8,128)} %matrix.1, f32[384,256]{1,0:T(8,128)} %panel_one.1, f32[384,256]{1,0:T(8,128)} %panel_two.1, s32[84,128]{1,0:T(8,128)} %bitcast.3, s32[72,128]{1,0:T(8,128)} %bitcast.4, ...), custom_call_target="tpu_custom_call" | custom-call | flops 14495514624 | bytes 18874368 | tf_op jit(solution)/shard_map/pallas_call | solution.py:905
  101.6 2.3 %shard_map.129 = (f32[384,256]{1,0:T(8,128)}, f32[256,256]{1,0:T(8,128)}, f32[256,256]{1,0:T(8,128)}, f32[256,256]{1,0:T(8,128)}, f32[8,64,256]{2,1,0:T(8,128)}) custom-call(f32[384,256]{1,0:T(8,128)} %get-tuple-element.10.refs_0_, f32[256,256]{1,0:T(8,128)} %get-tuple-element.11.refs_1_, f32[256,256]{1,0:T(8,128)} %get-tuple-element.12.refs_2_, ...), custom_call_target="tpu_custom_call" | custom-call | tf_op jit(solution)/shard_map/pallas_call | solution.py:989
